TPU v7x, 128 devices: a whole 4x4x4 slice. The times are simulated.
128 devices in a mesh: row: 8 (over y_lo, x), col: 8 (over y_hi, z), depth: 2 (over core).
Axes of the slice: x: 4, y: 4 (y_hi: 2, y_lo: 2; y = y_hi * 2 + y_lo), z: 4, core: 2. Of those that a mesh axis runs over, the one named last changes fastest.
Arguments:
- x_blocks: float32 [96, 32, 128, 128], P(('row', 'depth'), 'col'), may hold values from -1.2 to 1.2
- x_cols: int32 [96, 32], P(('row', 'depth'), 'col'), may hold values from 0 to 11, as said below
- c_cols: int32 [96, 32], P(('row', 'depth'), 'col'), may hold values from 0 to 11, as said below
Outputs:
- c_blocks: float32 [96, 32, 128, 128], P(('row', 'depth'), 'col')
Inputs may be any that keep to these rules, and one draw needn't show every extreme that they name: `x_cols`: within one block row and column tile the 4 entries are distinct. `c_cols`: within one block row and column tile the 4 entries are distinct.
All inputs are finite; a program needn't handle non-finite values.
Results may differ from a plain program's by a relative error of at most 0.0003.
Values sent between devices are 32-bit elements; how exact they have to be, the bound alone decides.
No kernel may reach another device: no remote copies, remote signals or barrier semaphores. Data moves between devices by JAX's collectives and lax.ppermute only.
A program may use at most 128 MiB of HBM per device.

v0:
```python
import jax
import jax.numpy as jnp
from jax import lax
from jax.sharding import PartitionSpec as P


def from_behind(value, axis, steps):
    count = lax.axis_size(axis)
    pairs = [(source, (source + steps) % count) for source in range(count)]
    return lax.ppermute(value, axis, pairs)


def block_product(left_blocks, left_cols, right_blocks, right_cols, out_cols):
    picked = jnp.take(right_blocks, left_cols, axis=0)
    picked_cols = jnp.take(right_cols, left_cols, axis=0)
    partial_prod = jnp.einsum(
        "isab,istbc->istac", left_blocks, picked, precision=lax.Precision.HIGHEST
    )
    matches = (picked_cols[:, :, :, None] == out_cols[:, None, None, :]).astype(jnp.float32)
    return jnp.einsum("istu,istac->iuac", matches, partial_prod, precision=lax.Precision.HIGHEST)


def align_left(operand, distance, loop_size):
    for bit_index in range(loop_size.bit_length() - 1):
        arrived = from_behind((operand[0], operand[1]), "col", 1 << bit_index)
        chosen = distance >> bit_index & 1 == 1
        operand = (
            jnp.where(chosen, arrived[0], operand[0]),
            jnp.where(chosen, arrived[1], operand[1]),
        )
    return operand


def align_right(operand, distance, loop_size):
    for bit_index in range(loop_size.bit_length() - 1):
        arrived = from_behind((operand[0], operand[1]), "row", 1 << bit_index)
        chosen = distance >> bit_index & 1 == 1
        operand = (
            jnp.where(chosen, arrived[0], operand[0]),
            jnp.where(chosen, arrived[1], operand[1]),
        )
    return operand


def per_device(x_blocks, x_cols, c_cols):
    loop_size = lax.axis_size("col")
    layer_count = lax.axis_size("depth")
    row_index = lax.axis_index("row")
    col_index = lax.axis_index("col")
    layer_index = lax.axis_index("depth")
    full_blocks, full_cols, full_kept = (
        lax.all_gather(x_blocks, "depth", axis=0, tiled=True),
        lax.all_gather(x_cols, "depth", axis=0, tiled=True),
        lax.all_gather(c_cols, "depth", axis=0, tiled=True),
    )
    turn_count = loop_size // layer_count
    offset = layer_index * turn_count
    left_pair = (full_blocks, full_cols)
    right_pair = (full_blocks, full_cols)
    left_pair = align_left(left_pair, (loop_size * 2 - row_index - offset) % loop_size, loop_size)
    right_pair = align_right(
        right_pair, (loop_size * 2 - col_index - offset) % loop_size, loop_size
    )
    product_sum = jnp.zeros(
        (full_kept.shape[0], full_kept.shape[1], x_blocks.shape[2], x_blocks.shape[3]), jnp.float32
    )
    for turn_index in range(turn_count):
        if turn_index > 0:
            left_pair = from_behind((left_pair[0], left_pair[1]), "col", -1)
            right_pair = from_behind((right_pair[0], right_pair[1]), "row", -1)
        product_sum = product_sum + block_product(
            left_pair[0], left_pair[1], right_pair[0], right_pair[1], full_kept
        )
    return lax.psum_scatter(product_sum, "depth", scatter_dimension=0, tiled=True)


def solution(mesh):
    return jax.shard_map(
        per_device,
        mesh=mesh,
        in_specs=(
            P(("row", "depth"), "col", None, None),
            P(("row", "depth"), "col"),
            P(("row", "depth"), "col"),
        ),
        out_specs=P(("row", "depth"), "col", None, None),
        check_vma=False,
    )
```

profile of v0, /device:TPU:1, one launch (start us, length us, event | category | flops | bytes accessed | tf_op | source)
XLA Modules:
  0.0 953.8 jit_solution(13097975956890675358)
XLA Ops:
  7.3 20.2 %all-gather.4.cloned.1.call-done = f32[12,4,128,128]{3,2,1,0:T(8,128)} async-done(((f32[6,4,128,128]{3,2,1,0:T(8,128)}), f32[12,4,128,128]{3,2,1,0:T(8,128)}) %all-gather.4.cloned.1.call-update) | async-done | bytes 3145744 | tf_op jit(solution)/shard_map/all_gather | solution.py:52
  30.0 138.4 %collective-permute-done.9 = f32[12,4,128,128]{3,2,1,0:T(8,128)S(1)} collective-permute-done((f32[12,4,128,128]{3,2,1,0:T(8,128)}, f32[12,4,128,128]{3,2,1,0:T(8,128)S(1)}, u32[]{:S(2)}, u32[]{:S(2)}) %collective-permute-start.9) | collective-permute-done | bytes 3145760 | tf_op jit(solution)/shard_map/ppermute | solution.py:10
  176.6 69.5 %collective-permute-done.7 = f32[12,4,128,128]{3,2,1,0:T(8,128)} collective-permute-done((f32[12,4,128,128]{3,2,1,0:T(8,128)S(1)}, f32[12,4,128,128]{3,2,1,0:T(8,128)}, u32[]{:S(2)}, u32[]{:S(2)}) %collective-permute-start.7) | collective-permute-done | bytes 3145760 | tf_op jit(solution)/shard_map/ppermute | solution.py:10
  256.2 60.4 %collective-permute-done.8 = f32[12,4,128,128]{3,2,1,0:T(8,128)} collective-permute-done((f32[12,4,128,128]{3,2,1,0:T(8,128)S(1)}, f32[12,4,128,128]{3,2,1,0:T(8,128)}, u32[]{:S(2)}, u32[]{:S(2)}) %collective-permute-start.8) | collective-permute-done | bytes 3145760 | tf_op jit(solution)/shard_map/ppermute | solution.py:10
  319.1 66.6 %collective-permute-done.11 = f32[12,4,128,128]{3,2,1,0:T(8,128)} collective-permute-done((f32[12,4,128,128]{3,2,1,0:T(8,128)}, f32[12,4,128,128]{3,2,1,0:T(8,128)}, u32[]{:S(2)}, u32[]{:S(2)}) %collective-permute-start.11) | collective-permute-done | bytes 3145760 | tf_op jit(solution)/shard_map/ppermute | solution.py:10
  389.9 62.0 %collective-permute-start.15 = (f32[12,4,128,128]{3,2,1,0:T(8,128)}, f32[12,4,128,128]{3,2,1,0:T(8,128)}, u32[]{:S(2)}, u32[]{:S(2)}) collective-permute-start(f32[12,4,128,128]{3,2,1,0:T(8,128)} %broadcast_select_fusion.2), channel_id=1, source_target_pairs={{0,14},{2,0},{4,2},{6,4},{8,6},{10,8},{12,10},{14,12},{1,15},{3,1}... | collective-permute-start | bytes 9437192 | tf_op jit(solution)/shard_map/ppermute | solution.py:10
  461.6 6.2 collective-permute-done.4
  469.3 50.2 %collective-permute-done.5 = s32[12,4]{0,1:T(4,128)S(1)} collective-permute-done((s32[12,4]{0,1:T(4,128)S(1)}, s32[12,4]{0,1:T(4,128)S(1)}, u32[]{:S(2)}, u32[]{:S(2)}) %collective-permute-start.5) | collective-permute-done | bytes 224 | tf_op jit(solution)/shard_map/ppermute | solution.py:10
  533.8 59.9 %collective-permute-done.21 = s32[12,4]{0,1:T(4,128)S(1)} collective-permute-done((s32[12,4]{0,1:T(4,128)S(1)}, s32[12,4]{0,1:T(4,128)S(1)}, u32[]{:S(2)}, u32[]{:S(2)}) %collective-permute-start.21) | collective-permute-done | bytes 224 | tf_op jit(solution)/shard_map/ppermute | solution.py:10
  594.7 5.9 gather_fusion.1
  600.6 12.6 %copy.57 = f32[12,4,4,128,128]{3,4,2,1,0:T(8,128)} copy(f32[12,4,4,128,128]{4,3,2,1,0:T(8,128)} %bitcast.82) | data formatting | bytes 25165824 | tf_op jit(solution)/shard_map/jit(_take)/gather | solution.py:14
  613.3 16.3 %fusion.16 = f32[12,4,4,128,128]{3,4,2,1,0:T(8,128)} fusion(f32[12,4,4,128,128]{3,4,2,1,0:T(8,128)} %copy.57, pred[12,4]{1,0:T(8,128)(4,1)S(1)} %copy.49, f32[12,4,128,128]{3,2,1,0:T(8,128)} %broadcast_select_fusion.2), kind=kOutput, calls=%fused_computation.24 | convolution fusion | flops 4834983936 | bytes 28311600 | tf_op jit(solution)/shard_map/isab,istbc->istac/dot_general | solution.py:16
  629.6 15.1 %copy.58 = f32[12,4,4,128,128]{4,2,1,3,0:T(4,128)} copy(f32[12,4,4,128,128]{3,4,2,1,0:T(8,128)} %fusion.16) | data formatting | bytes 25165824 | tf_op jit(solution)/shard_map/isab,istbc->istac/transpose | solution.py:16
  644.6 14.3 %fusion.37 = f32[12,4,128,128,1]{3,1,4,2,0:T(4,128)} fusion(f32[12,4,4,128,128]{4,2,1,3,0:T(4,128)} %copy.58, s32[12,4]{1,0:T(8,128)S(1)} %copy.54, s32[12,4,4]{2,1,0:T(4,128)S(1)} %broadcast_select_fusion.9), kind=kOutput, calls=%fused_computation.46 | convolution fusion | flops 150995712 | bytes 15729600 | tf_op jit(solution)/shard_map/istu,istac->iuac/dot_general | solution.py:20
  659.0 9.4 gather_fusion.3
  668.4 12.6 %copy.63 = f32[12,4,4,128,128]{3,4,2,1,0:T(8,128)} copy(f32[12,4,4,128,128]{4,3,2,1,0:T(8,128)} %bitcast.84) | data formatting | bytes 25165824 | tf_op jit(solution)/shard_map/jit(_take)/gather | solution.py:14
  681.1 64.5 %collective-permute-start.22 = (f32[12,4,128,128]{3,2,1,0:T(8,128)}, f32[12,4,128,128]{3,2,1,0:T(8,128)S(1)}, u32[]{:S(2)}, u32[]{:S(2)}) collective-permute-start(f32[12,4,128,128]{3,2,1,0:T(8,128)} %collective-permute-done.18), channel_id=1, source_target_pairs={{0,112},{16,0},{32,16},{48,32},{64,48},{80,64},{96,80},{112,96},{1... | collective-permute-start | bytes 9437192 | tf_op jit(solution)/shard_map/ppermute | solution.py:10
  745.6 6.4 collective-permute-start.23
  752.0 16.3 %fusion.19 = f32[12,4,4,128,128]{3,4,2,1,0:T(8,128)} fusion(f32[12,4,4,128,128]{3,4,2,1,0:T(8,128)} %copy.63, pred[12,4]{1,0:T(8,128)(4,1)S(1)} %copy.59, f32[12,4,128,128]{3,2,1,0:T(8,128)} %collective-permute-done.15), kind=kOutput, calls=%fused_computation.25 | convolution fusion | flops 4834983936 | bytes 28311600 | tf_op jit(solution)/shard_map/isab,istbc->istac/dot_general | solution.py:16
  768.3 15.1 %copy.64 = f32[12,4,4,128,128]{4,2,1,3,0:T(4,128)} copy(f32[12,4,4,128,128]{3,4,2,1,0:T(8,128)} %fusion.19) | data formatting | bytes 25165824 | tf_op jit(solution)/shard_map/isab,istbc->istac/transpose | solution.py:16
  783.3 14.3 %fusion.35 = f32[12,4,128,128,1]{3,1,4,2,0:T(4,128)} fusion(f32[12,4,4,128,128]{4,2,1,3,0:T(4,128)} %copy.64, s32[12,4,4]{2,1,0:T(4,128)S(1)} %broadcast_select_fusion.8, s32[12,4]{1,0:T(8,128)S(1)} %copy.54), kind=kOutput, calls=%fused_computation.44 | convolution fusion | flops 150995712 | bytes 15729600 | tf_op jit(solution)/shard_map/istu,istac->iuac/dot_general | solution.py:20
  797.7 9.5 gather_fusion.5
  807.1 12.6 %copy.69 = f32[12,4,4,128,128]{3,4,2,1,0:T(8,128)} copy(f32[12,4,4,128,128]{4,3,2,1,0:T(8,128)} %bitcast.85) | data formatting | bytes 25165824 | tf_op jit(solution)/shard_map/jit(_take)/gather | solution.py:14
  819.8 16.5 %fusion.22 = f32[12,4,4,128,128]{3,4,2,1,0:T(8,128)} fusion(f32[12,4,4,128,128]{3,4,2,1,0:T(8,128)} %copy.69, pred[12,4]{1,0:T(8,128)(4,1)S(1)} %copy.65, f32[12,4,128,128]{3,2,1,0:T(8,128)} %collective-permute-done.19), kind=kOutput, calls=%fused_computation.26 | convolution fusion | flops 4834983936 | bytes 28311600 | tf_op jit(solution)/shard_map/isab,istbc->istac/dot_general | solution.py:16
  836.3 15.1 %copy.70 = f32[12,4,4,128,128]{4,2,1,3,0:T(4,128)} copy(f32[12,4,4,128,128]{3,4,2,1,0:T(8,128)} %fusion.22) | data formatting | bytes 25165824 | tf_op jit(solution)/shard_map/isab,istbc->istac/transpose | solution.py:16
  851.3 14.4 %fusion.33 = f32[12,4,128,128,1]{3,1,4,2,0:T(4,128)} fusion(f32[12,4,4,128,128]{4,2,1,3,0:T(4,128)} %copy.70, s32[12,4,4]{2,1,0:T(4,128)S(1)} %broadcast_select_fusion.7, s32[12,4]{1,0:T(8,128)S(1)} %copy.54), kind=kOutput, calls=%fused_computation.42 | convolution fusion | flops 150995712 | bytes 15729600 | tf_op jit(solution)/shard_map/istu,istac->iuac/dot_general | solution.py:20
  865.7 5.9 gather_fusion.7
  871.6 12.6 %copy.75 = f32[12,4,4,128,128]{3,4,2,1,0:T(8,128)} copy(f32[12,4,4,128,128]{4,3,2,1,0:T(8,128)} %bitcast.83) | data formatting | bytes 25165824 | tf_op jit(solution)/shard_map/jit(_take)/gather | solution.py:14
  884.3 16.6 %fusion.25 = f32[12,4,4,128,128]{3,4,2,1,0:T(8,128)} fusion(f32[12,4,4,128,128]{3,4,2,1,0:T(8,128)} %copy.75, pred[12,4]{1,0:T(8,128)(4,1)S(1)} %copy.71, f32[12,4,128,128]{3,2,1,0:T(8,128)} %collective-permute-done.23), kind=kOutput, calls=%fused_computation.27 | convolution fusion | flops 4834983936 | bytes 28311600 | tf_op jit(solution)/shard_map/isab,istbc->istac/dot_general | solution.py:16
  900.8 15.2 %copy.76 = f32[12,4,4,128,128]{4,2,1,3,0:T(4,128)} copy(f32[12,4,4,128,128]{3,4,2,1,0:T(8,128)} %fusion.25) | data formatting | bytes 25165824 | tf_op jit(solution)/shard_map/isab,istbc->istac/transpose | solution.py:16
  916.0 14.6 %bitcast_add_fusion = f32[12,4,128,128]{3,1,2,0:T(4,128)S(1)} fusion(f32[12,4,128,128,1]{3,1,4,2,0:T(4,128)} %fusion.33, f32[12,4,128,128,1]{3,1,4,2,0:T(4,128)} %fusion.35, f32[12,4,128,128,1]{3,1,4,2,0:T(4,128)S(1)} %copy-done, f32[12,4,4,128,128]{4,2,1,3,0:T(4,128)} %copy.76, s32[12,4,4]{2,1,0:T(4,128)S(1)} %broadcast_select_fusion.6, s32[12,4]{1,0:T(8,128)S(1)} %copy.54), kind=kOutput, calls=%fused_computation.32 | convolution fusion | flops 153355008 | bytes 25166784 | tf_op jit(solution)/shard_map/istu,istac->iuac/dot_general | solution.py:20
  932.7 13.7 %reduce-scatter.2.cloned.1.call-done = f32[6,4,128,128]{3,2,1,0:T(8,128)} async-done(((f32[12,4,128,128]{3,2,1,0:T(8,128)}), f32[6,4,128,128]{3,2,1,0:T(8,128)}) %reduce-scatter.2.cloned.1.call-update) | async-done | bytes 1572880 | tf_op jit(solution)/shard_map/reduce_scatter | solution.py:74
  (105 shorter events, 56.6 us)
Async XLA Ops:
  6.5 20.9 %all-gather.4.cloned.1.call-start = ((), (), s32[]{:S(2)}) async-start(), calls=%async_computation.1 | async-start | bytes 4718592 | tf_op jit(solution)/shard_map/all_gather | solution.py:52
  7.3 939.2 %reduce-scatter.2.cloned.1.call-start = ((), (), s32[]{:S(2)}) async-start(), calls=%async_computation.2 | async-start | bytes 4718592 | tf_op jit(solution)/shard_map/reduce_scatter | solution.py:74
  27.5 141.0 %collective-permute-start.9 = (f32[12,4,128,128]{3,2,1,0:T(8,128)}, f32[12,4,128,128]{3,2,1,0:T(8,128)S(1)}, u32[]{:S(2)}, u32[]{:S(2)}) collective-permute-start(f32[12,4,128,128]{3,2,1,0:T(8,128)} %all-gather.4.cloned.1.call-done), channel_id=1, source_target_pairs={{0,2},{2,4},{4,6},{6,8},{8,10},{10,12},{12,14},{14,0},{1,3},{3,5},... | collective-permute-start | bytes 9437192 | tf_op jit(solution)/shard_map/ppermute | solution.py:10
  28.8 141.3 %collective-permute-start.6 = (f32[12,4,128,128]{3,2,1,0:T(8,128)}, f32[12,4,128,128]{3,2,1,0:T(8,128)}, u32[]{:S(2)}, u32[]{:S(2)}) collective-permute-start(f32[12,4,128,128]{3,2,1,0:T(8,128)} %all-gather.4.cloned.1.call-done), channel_id=1, source_target_pairs={{0,16},{16,32},{32,48},{48,64},{64,80},{80,96},{96,112},{112,0},{1... | collective-permute-start | bytes 9437192 | tf_op jit(solution)/shard_map/ppermute | solution.py:10
  168.4 1.7 copy-start.3
  174.9 1.7 copy-start.2
  174.9 71.2 %collective-permute-start.7 = (f32[12,4,128,128]{3,2,1,0:T(8,128)S(1)}, f32[12,4,128,128]{3,2,1,0:T(8,128)}, u32[]{:S(2)}, u32[]{:S(2)}) collective-permute-start(f32[12,4,128,128]{3,2,1,0:T(8,128)S(1)} %get-tuple-element.10), channel_id=1, source_target_pairs={{0,32},{16,48},{32,64},{48,80},{64,96},{80,112},{96,0},{112,16},{1... | collective-permute-start | bytes 9437192 | tf_op jit(solution)/shard_map/ppermute | solution.py:10
  174.9 74.6 %collective-permute-start.10 = (f32[12,4,128,128]{3,2,1,0:T(8,128)}, f32[12,4,128,128]{3,2,1,0:T(8,128)}, u32[]{:S(2)}, u32[]{:S(2)}) collective-permute-start(f32[12,4,128,128]{3,2,1,0:T(8,128)} %get-tuple-element.9), channel_id=1, source_target_pairs={{0,4},{2,6},{4,8},{6,10},{8,12},{10,14},{12,0},{14,2},{1,5},{3,7},... | collective-permute-start | bytes 9437192 | tf_op jit(solution)/shard_map/ppermute | solution.py:10
  248.5 5.3 copy-start.1
  248.5 68.1 %collective-permute-start.8 = (f32[12,4,128,128]{3,2,1,0:T(8,128)S(1)}, f32[12,4,128,128]{3,2,1,0:T(8,128)}, u32[]{:S(2)}, u32[]{:S(2)}) collective-permute-start(f32[12,4,128,128]{3,2,1,0:T(8,128)S(1)} %broadcast_select_fusion.4), channel_id=1, source_target_pairs={{0,64},{16,80},{32,96},{48,112},{64,0},{80,16},{96,32},{112,48},{1... | collective-permute-start | bytes 9437192 | tf_op jit(solution)/shard_map/ppermute | solution.py:10
  253.8 131.9 %collective-permute-start.11 = (f32[12,4,128,128]{3,2,1,0:T(8,128)}, f32[12,4,128,128]{3,2,1,0:T(8,128)}, u32[]{:S(2)}, u32[]{:S(2)}) collective-permute-start(f32[12,4,128,128]{3,2,1,0:T(8,128)} %broadcast_select_fusion.1), channel_id=1, source_target_pairs={{0,8},{2,10},{4,12},{6,14},{8,0},{10,2},{12,4},{14,6},{1,9},{3,11}... | collective-permute-start | bytes 9437192 | tf_op jit(solution)/shard_map/ppermute | solution.py:10
  319.0 133.0 %copy-start.4 = (s32[6,4]{0,1:T(4,128)S(1)}, s32[6,4]{0,1:T(4,128)}, u32[]{:S(2)}) copy-start(s32[6,4]{0,1:T(4,128)} %param.8) | copy-start | bytes 292
  319.0 136.6 %copy-start.5 = (s32[6,4]{0,1:T(4,128)S(1)}, s32[6,4]{0,1:T(4,128)}, u32[]{:S(2)}) copy-start(s32[6,4]{0,1:T(4,128)} %param.9) | copy-start | bytes 292
  319.0 208.0 %collective-permute-start.14 = (f32[12,4,128,128]{3,2,1,0:T(8,128)S(1)}, f32[12,4,128,128]{3,2,1,0:T(8,128)}, u32[]{:S(2)}, u32[]{:S(2)}) collective-permute-start(f32[12,4,128,128]{3,2,1,0:T(8,128)S(1)} %broadcast_select_fusion.5), channel_id=1, source_target_pairs={{0,112},{16,0},{32,16},{48,32},{64,48},{80,64},{96,80},{112,96},{1... | collective-permute-start | bytes 9437192 | tf_op jit(solution)/shard_map/ppermute | solution.py:10
  389.9 137.2 %collective-permute-start.15 = (f32[12,4,128,128]{3,2,1,0:T(8,128)}, f32[12,4,128,128]{3,2,1,0:T(8,128)}, u32[]{:S(2)}, u32[]{:S(2)}) collective-permute-start(f32[12,4,128,128]{3,2,1,0:T(8,128)} %broadcast_select_fusion.2), channel_id=1, source_target_pairs={{0,14},{2,0},{4,2},{6,4},{8,6},{10,8},{12,10},{14,12},{1,15},{3,1}... | collective-permute-start | bytes 9437192 | tf_op jit(solution)/shard_map/ppermute | solution.py:10
  455.4 6.0 collective-permute-start.3
  455.5 6.0 collective-permute-start
  461.5 6.3 collective-permute-start.4
  461.5 6.7 collective-permute-start.1
  467.8 51.6 %collective-permute-start.5 = (s32[12,4]{0,1:T(4,128)S(1)}, s32[12,4]{0,1:T(4,128)S(1)}, u32[]{:S(2)}, u32[]{:S(2)}) collective-permute-start(s32[12,4]{0,1:T(4,128)S(1)} %broadcast_select_fusion.14), channel_id=1, source_target_pairs={{0,8},{2,10},{4,12},{6,14},{8,0},{10,2},{12,4},{14,6},{1,9},{3,11}... | collective-permute-start | bytes 584 | tf_op jit(solution)/shard_map/ppermute | solution.py:10
  468.3 51.3 %collective-permute-start.2 = (s32[12,4]{1,0:T(8,128)S(1)}, s32[12,4]{1,0:T(8,128)S(1)}, u32[]{:S(2)}, u32[]{:S(2)}) collective-permute-start(s32[12,4]{1,0:T(8,128)S(1)} %broadcast_select_fusion.11), channel_id=1, source_target_pairs={{0,64},{16,80},{32,96},{48,112},{64,0},{80,16},{96,32},{112,48},{1... | collective-permute-start | bytes 584 | tf_op jit(solution)/shard_map/ppermute | solution.py:10
  519.5 2.5 collective-permute-start.13
  519.6 6.8 collective-permute-start.12
  522.3 5.0 collective-permute-start.17
  526.3 6.4 collective-permute-start.16
  527.0 154.0 %collective-permute-start.18 = (f32[12,4,128,128]{3,2,1,0:T(8,128)}, f32[12,4,128,128]{3,2,1,0:T(8,128)}, u32[]{:S(2)}, u32[]{:S(2)}) collective-permute-start(f32[12,4,128,128]{3,2,1,0:T(8,128)} %collective-permute-done.14), channel_id=1, source_target_pairs={{0,112},{16,0},{32,16},{48,32},{64,48},{80,64},{96,80},{112,96},{1... | collective-permute-start | bytes 9437192 | tf_op jit(solution)/shard_map/ppermute | solution.py:10
  527.1 218.4 %collective-permute-start.19 = (f32[12,4,128,128]{3,2,1,0:T(8,128)}, f32[12,4,128,128]{3,2,1,0:T(8,128)}, u32[]{:S(2)}, u32[]{:S(2)}) collective-permute-start(f32[12,4,128,128]{3,2,1,0:T(8,128)} %collective-permute-done.15), channel_id=1, source_target_pairs={{0,14},{2,0},{4,2},{6,4},{8,6},{10,8},{12,10},{14,12},{1,15},{3,1}... | collective-permute-start | bytes 9437192 | tf_op jit(solution)/shard_map/ppermute | solution.py:10
  527.6 66.1 %collective-permute-start.21 = (s32[12,4]{0,1:T(4,128)S(1)}, s32[12,4]{0,1:T(4,128)S(1)}, u32[]{:S(2)}, u32[]{:S(2)}) collective-permute-start(s32[12,4]{0,1:T(4,128)S(1)} %collective-permute-done.17), channel_id=1, source_target_pairs={{0,14},{2,0},{4,2},{6,4},{8,6},{10,8},{12,10},{14,12},{1,15},{3,1}... | collective-permute-start | bytes 584 | tf_op jit(solution)/shard_map/ppermute | solution.py:10
  533.4 60.7 %collective-permute-start.20 = (s32[12,4]{1,0:T(8,128)S(1)}, s32[12,4]{1,0:T(8,128)S(1)}, u32[]{:S(2)}, u32[]{:S(2)}) collective-permute-start(s32[12,4]{1,0:T(8,128)S(1)} %collective-permute-done.16), channel_id=1, source_target_pairs={{0,112},{16,0},{32,16},{48,32},{64,48},{80,64},{96,80},{112,96},{1... | collective-permute-start | bytes 584 | tf_op jit(solution)/shard_map/ppermute | solution.py:10
  681.1 184.7 %collective-permute-start.22 = (f32[12,4,128,128]{3,2,1,0:T(8,128)}, f32[12,4,128,128]{3,2,1,0:T(8,128)S(1)}, u32[]{:S(2)}, u32[]{:S(2)}) collective-permute-start(f32[12,4,128,128]{3,2,1,0:T(8,128)} %collective-permute-done.18), channel_id=1, source_target_pairs={{0,112},{16,0},{32,16},{48,32},{64,48},{80,64},{96,80},{112,96},{1... | collective-permute-start | bytes 9437192 | tf_op jit(solution)/shard_map/ppermute | solution.py:10
  745.6 138.7 %collective-permute-start.23 = (f32[12,4,128,128]{3,2,1,0:T(8,128)}, f32[12,4,128,128]{3,2,1,0:T(8,128)}, u32[]{:S(2)}, u32[]{:S(2)}) collective-permute-start(f32[12,4,128,128]{3,2,1,0:T(8,128)} %collective-permute-done.19), channel_id=1, source_target_pairs={{0,14},{2,0},{4,2},{6,4},{8,6},{10,8},{12,10},{14,12},{1,15},{3,1}... | collective-permute-start | bytes 9437192 | tf_op jit(solution)/shard_map/ppermute | solution.py:10
  900.8 15.2 %copy-start = (f32[12,4,128,128,1]{3,1,4,2,0:T(4,128)S(1)}, f32[12,4,128,128,1]{3,1,4,2,0:T(4,128)}, u32[]{:S(2)}) copy-start(f32[12,4,128,128,1]{3,1,4,2,0:T(4,128)} %fusion.37) | copy-start | bytes 9437188
Sparse Core Ops, SparseCore 0:
  9.0 18.4 all-gather.3
  932.9 13.5 reduce-scatter.1
where the time goes:
time: 964 us; the launch traced here: 954 us
  waiting for transfers between devices  491 us (51%)
  local copies, waits for them, and re-layouts  151 us (16%)
  starting transfers between devices  150 us (16%)
  matrix products  123 us (13%)
  other arithmetic  18.4 us (2%)
  between operations  14.1 us (1%)
    ppermute x24, waiting for transfers between devices, from_behind(): return lax.ppermute(value, axis, pairs)  457 us
    ppermute x24, starting transfers between devices, from_behind(): return lax.ppermute(value, axis, pairs)  150 us
    gather x8, local copies, waits for them, and re-layouts, block_product(): picked = jnp.take(right_blocks, left_cols, axis=0)  81.3 us
    dot_general x4, matrix products, block_product(): jnp.einsum('isab,istbc->istac', left_blocks, picked, precision=lax.Precis...  65.7 us
    transpose x4, local copies, waits for them, and re-layouts, block_product(): jnp.einsum('isab,istbc->istac', left_blocks, picked, precision=lax.Precis...  60.4 us
    dot_general x4, matrix products, block_product(): jnp.einsum('istu,istac->iuac', matches, partial_prod, precision=lax.Preci...  57.7 us
    all_gather x1, waiting for transfers between devices, per_device(): lax.all_gather(x_blocks, 'depth', axis=0, tiled=True)  20.2 us
  transfers between devices with their start and end apart: 26, of which 11 were waited for; matrix products, arithmetic and copies ran while one was open for 25% of the time, Pallas kernels for 0%

commit v1 on v0

v1 whole, which is shorter than its diff:
```python
import functools

import jax
import jax.numpy as jnp
import numpy as np
from jax import lax
from jax.experimental import pallas as pl
from jax.experimental.pallas import tpu as pltpu
from jax.sharding import PartitionSpec as P


AXES = ("row", "col", "depth")
RING = 4
HALF = 6
SLOTS = 4
BS = 128
ROWS = HALF * SLOTS * BS
EXTRA = 8
GROUP = 8
TRASH = HALF * SLOTS
F32, BF16 = jnp.float32, jnp.bfloat16


def device_number(x, y, z, d):
    y_hi, y_lo = y >> 1, y & 1
    return (y_lo * RING + x) * 16 + (y_hi * RING + z) * 2 + d


def all_places():
    return [(x, y, z, d) for x in range(4) for y in range(4) for z in range(4) for d in range(2)]


def move(value, dx=0, dz=0, y_flip=0, d_flip=0):
    pairs = [
        (
            device_number(x, y, z, d),
            device_number((x + dx) % 4, y ^ y_flip, (z + dz) % 4, d ^ d_flip),
        )
        for x, y, z, d in all_places()
    ]
    return lax.ppermute(value, AXES, pairs)


STAGE = (0, 0, 0, 0, 0, 1, 1, 2)


def panel_table():
    table = np.zeros((128, 3, 17), np.int32)
    for x, y, z, d in all_places():
        rows = table[device_number(x, y, z, d)]
        for h in range(2):
            for w in range(4):
                left = 4 * (h != y >> 1) + (0, 2, 3, 1)[(w - z) % 4]
                right = 4 * (h != (y & 1)) + (0, 2, 3, 1)[(w - x) % 4]
                row = rows[max(STAGE[left], STAGE[right])]
                row[1 + 2 * row[0]] = left
                row[2 + 2 * row[0]] = right
                row[0] += 1
    return table


def split(value):
    high = value.astype(BF16)
    return high, (value - high.astype(F32)).astype(BF16)


def product(a, b):
    a_high, a_low = split(a)
    b_high, b_low = split(b)
    side = jnp.concatenate([b_high, b_low], 1)
    both = jnp.dot(
        jnp.concatenate([a_high, a_low], 1),
        jnp.concatenate([side, side], 0),
        preferred_element_type=F32,
    )
    return both[:, :BS] + both[:, BS:]


def gate_kernel(a_ref, o_ref):
    for i in range(3):
        for j in range(17):
            o_ref[i, j] = a_ref[i, j]


def gate(meta):
    return pl.pallas_call(
        gate_kernel,
        out_shape=jax.ShapeDtypeStruct((3, 17), jnp.int32),
        in_specs=[pl.BlockSpec(memory_space=pltpu.SMEM)],
        out_specs=pl.BlockSpec(memory_space=pltpu.SMEM),
        cost_estimate=pl.CostEstimate(flops=100, bytes_accessed=1000, transcendentals=0),
    )(meta)


def panels_kernel(stage, lefts, rights, first, n_refs, depth_ref, meta_ref, kept_ref, *refs):
    pieces = refs[:n_refs]
    at = n_refs
    before = None
    if not first:
        before = refs[at]
        at += 1
    out, lb, rb, cb, lc, rc, inv, lst, sem, csem = refs[at:]
    depth = depth_ref[0]
    count = meta_ref[stage, 0]
    whole = pl.ds(0, ROWS)

    def copies(j, sources, dst, cols, data_sem, col_sem):
        for ref, src, rows, to, has_cols in sources[j]:
            pltpu.make_async_copy(
                pieces[ref].at[pl.ds(src, rows)], dst.at[pl.ds(to, rows)], data_sem
            ).start()
            if has_cols:
                pltpu.make_async_copy(
                    pieces[ref].at[pl.ds(src + rows, EXTRA)], cols, col_sem
                ).start()

    def fetch(n, slot):
        left, right = meta_ref[stage, 1 + 2 * n], meta_ref[stage, 2 + 2 * n]
        for j in lefts:
            @pl.when(left == j)
            def _():
                copies(j, lefts, lb.at[slot], lc.at[slot], sem.at[slot, 0], csem.at[slot, 0])
        for j in rights:
            @pl.when(right == j)
            def _():
                for mine in range(2):
                    half = depth if mine == 0 else 1 - depth
                    copies(
                        (j, mine),
                        rights[j],
                        rb.at[slot, pl.ds(pl.multiple_of(half * ROWS, ROWS), ROWS)],
                        rc.at[slot, half],
                        sem.at[slot, 1 + mine],
                        csem.at[slot, 1 + mine],
                    )

    @pl.when(count > 0)
    def _():
        fetch(0, 0)

    if first:
        cb[...] = jnp.zeros_like(cb)
    else:
        load = pltpu.make_async_copy(before, cb.at[whole], sem.at[0, 3])
        load.start()

    def clear(n, carry):
        inv[n] = -1
        return carry

    lax.fori_loop(0, HALF * 16, clear, 0)
    for i in range(HALF):
        for u in range(SLOTS):
            inv[i * 16 + kept_ref[i, u]] = u
    if not first:
        load.wait()

    def panel(n, carry):
        slot = lax.rem(n, 2)

        @pl.when(n + 1 < count)
        def _():
            fetch(n + 1, 1 - slot)

        pltpu.make_async_copy(lc.at[slot], lc.at[slot], csem.at[slot, 0]).wait()
        for mine in range(2):
            pltpu.make_async_copy(rc.at[slot, 0], rc.at[slot, 0], csem.at[slot, 1 + mine]).wait()

        def list_row(e, total):
            i = e // SLOTS
            k = lc[slot, 0, e].astype(jnp.int32)
            half = (k >= HALF).astype(jnp.int32)
            base = (k - HALF * half) * SLOTS
            code = e + k * 256
            for t in range(SLOTS):
                column = rc[slot, half, 0, base + t].astype(jnp.int32)
                u = inv[i * 16 + column]
                lst[total] = code + t * 64 + (i * SLOTS + u) * 4096
                total = total + (u >= 0).astype(jnp.int32)
            return total

        total = lax.fori_loop(0, HALF * SLOTS, list_row, 0)
        for q in range(GROUP):
            lst[total + q] = TRASH * 4096
        pltpu.make_async_copy(lb.at[slot], lb.at[slot], sem.at[slot, 0]).wait()
        for mine in range(2):
            pltpu.make_async_copy(
                rb.at[slot, whole], rb.at[slot, whole], sem.at[slot, 1 + mine]
            ).wait()

        def group(g, carry):
            done = []
            for q in range(GROUP):
                code = lst[g * GROUP + q]
                a = pl.multiple_of((code & 63) * BS, BS)
                b = pl.multiple_of(((code >> 6) & 63) * BS, BS)
                c = pl.multiple_of((code >> 12) * BS, BS)
                done.append((c, product(lb[slot, pl.ds(a, BS)], rb[slot, pl.ds(b, BS)])))
            for c, value in done:
                cb[pl.ds(c, BS)] += value
            return carry

        lax.fori_loop(0, (total + GROUP - 1) // GROUP, group, 0)
        return carry

    lax.fori_loop(0, count, panel, 0)
    store = pltpu.make_async_copy(cb.at[whole], out, sem.at[0, 3])
    store.start()
    store.wait()


def add_panels(stage, lefts, rights, before, depth, meta, kept, panels):
    arrays, numbers = [], {}

    def numbered(pieces):
        out = []
        for array, *rest in pieces:
            if id(array) not in numbers:
                numbers[id(array)] = len(arrays)
                arrays.append(array)
            out.append((numbers[id(array)], *rest))
        return out

    left_refs = {j: numbered(p) for j, p in lefts.items()}
    right_refs = {j: {k: numbered(p) for k, p in both.items()} for j, both in rights.items()}
    first = before is None
    body = functools.partial(panels_kernel, stage, left_refs, right_refs, first, len(arrays))
    smem = pl.BlockSpec(memory_space=pltpu.SMEM)
    hbm = pl.BlockSpec(memory_space=pl.ANY)
    args = arrays + ([] if first else [before])
    return pl.pallas_call(
        body,
        out_shape=jax.ShapeDtypeStruct((ROWS, BS), F32),
        in_specs=[smem] * 3 + [hbm] * len(args),
        out_specs=hbm,
        scratch_shapes=[
            pltpu.VMEM((2, ROWS, BS), F32),
            pltpu.VMEM((2, 2 * ROWS, BS), F32),
            pltpu.VMEM((ROWS + BS, BS), F32),
            pltpu.SMEM((2, EXTRA, BS), F32),
            pltpu.SMEM((2, 2, EXTRA, BS), F32),
            pltpu.SMEM((HALF * 16,), jnp.int32),
            pltpu.SMEM((HALF * SLOTS * SLOTS + GROUP,), jnp.int32),
            pltpu.SemaphoreType.DMA((2, 4)),
            pltpu.SemaphoreType.DMA((2, 3)),
        ],
        compiler_params=pltpu.CompilerParams(vmem_limit_bytes=16 << 20),
        cost_estimate=pl.CostEstimate(
            flops=panels * 400_000_000, bytes_accessed=panels * 5_000_000, transcendentals=0
        ),
    )(depth, meta, kept, *args)


def whole_piece(array):
    return [(array, 0, ROWS, 0, True)]


CUT = ROWS // 2


def half_pieces(front, back):
    return [(front, 0, CUT, 0, False), (back, 0, ROWS - CUT, CUT, True)]


def per_device(x_blocks, x_cols, c_cols):
    place = lax.axis_index(AXES)
    depth = lax.axis_index("depth").astype(jnp.int32).reshape(1)
    meta = lax.dynamic_index_in_dim(jnp.asarray(panel_table()), place, 0, keepdims=False)
    columns = jnp.pad(x_cols.reshape(1, HALF * SLOTS).astype(F32), ((0, EXTRA - 1), (0, BS - HALF * SLOTS)))
    own = jnp.concatenate([x_blocks.reshape(ROWS, BS), columns], 0)
    y1, y2 = move(own, y_flip=1), move(own, y_flip=2)
    swap = lambda value: move(value, d_flip=1)

    def ring(tile, axis):
        step = {axis: 1}, {axis: -1}
        behind, ahead = move(tile, **step[0]), move(tile, **step[1])
        front = move(behind[:CUT], **step[0])
        back = move(ahead[CUT:], **step[1])
        return [[tile], [behind], [ahead], [front, back]]

    def pieces(arrays):
        return whole_piece(arrays[0]) if len(arrays) == 1 else half_pieces(*arrays)

    left_sources = ring(own, "dz") + ring(y2, "dz")
    right_sources = ring(own, "dx") + ring(y1, "dx")
    lefts = {j: pieces(s) for j, s in enumerate(left_sources)}
    rights = {
        j: {
            (j, 0): pieces(s),
            (j, 1): pieces([swap(v) for v in s]),
        }
        for j, s in enumerate(right_sources)
    }
    meta = gate(gate(meta))
    total = None
    for stage, panels in enumerate((3, 3, 2)):
        there = [j for j in range(8) if STAGE[j] <= stage]
        total = add_panels(
            stage,
            {j: lefts[j] for j in there},
            {j: rights[j] for j in there},
            total,
            depth,
            meta,
            c_cols,
            panels,
        )
    return total.reshape(HALF, SLOTS, BS, BS)


def solution(mesh):
    return jax.shard_map(
        per_device,
        mesh=mesh,
        in_specs=(
            P(("row", "depth"), "col", None, None),
            P(("row", "depth"), "col"),
            P(("row", "depth"), "col"),
        ),
        out_specs=P(("row", "depth"), "col", None, None),
        check_vma=False,
    )
```

time: 964 us -> 224 us (0.23)
  waiting for transfers between devices: 491 us -> 101 us
  matrix products: 123 us -> 0 us
  local copies, waits for them, and re-layouts: 151 us -> 37.9 us
  starting transfers between devices: 150 us -> 49.7 us
  Pallas kernels: 0 us -> 32.1 us
  other arithmetic: 18.4 us -> 2.19 us
  between operations: 14.1 us -> 0.46 us
    ppermute x24 -> x28, waiting for transfers between devices: 457 us -> 101 us  [move(): return lax.ppermute(value, AXES, pairs)]
    dot_general x8 -> x0, matrix products: 123 us -> none  [the longest x4 65.7 us: block_product(): jnp.einsum('isab,istbc->istac', left_blocks, picked, precision=lax.Precis...]
    ppermute x24 -> x28, starting transfers between devices: 150 us -> 49.7 us  [move(): return lax.ppermute(value, AXES, pairs)]
    gather x12 -> x0, local copies, waits for them, and re-layouts: 83.6 us -> none  [the longest x8 81.3 us: block_product(): picked = jnp.take(right_blocks, left_cols, axis=0)]
    transpose x4 -> x0, local copies, waits for them, and re-layouts: 60.4 us -> none  [block_product(): jnp.einsum('isab,istbc->istac', left_blocks, picked, precision=lax.Precis...]
    pallas_call x0 -> x5, Pallas kernels: none -> 32.1 us  [the longest x3 29.5 us: add_panels(): pl.pallas_call(body, out_shape=jax.ShapeDtypeStruct((ROWS, BS), F32), in_...]
    unnamed x16 -> x81, local copies, waits for them, and re-layouts: 3.77 us -> 33.1 us
    all_gather x1 -> x0, waiting for transfers between devices: 20.2 us -> none  [per_device(): lax.all_gather(x_blocks, 'depth', axis=0, tiled=True)]
  transfers between devices with their start and end apart: 26 -> 28, of which waited for: 11 -> 9; matrix products, arithmetic and copies ran while one was open for 25% -> 2% of each run, Pallas kernels for 0% -> 12%
where the time goes in v1:
time: 224 us; the launch traced here: 223 us
  waiting for transfers between devices  101 us (45%)
  starting transfers between devices  49.7 us (22%)
  local copies, waits for them, and re-layouts  37.9 us (17%)
  Pallas kernels  32.1 us (14%)
    ppermute x28, waiting for transfers between devices, move(): return lax.ppermute(value, AXES, pairs)  101 us
    ppermute x28, starting transfers between devices, move(): return lax.ppermute(value, AXES, pairs)  49.7 us
    unnamed x81, local copies, waits for them, and re-layouts  33.1 us
    pallas_call x3, Pallas kernels, add_panels(): pl.pallas_call(body, out_shape=jax.ShapeDtypeStruct((ROWS, BS), F32), in_...  29.5 us
  transfers between devices with their start and end apart: 28, of which 9 were waited for; matrix products, arithmetic and copies ran while one was open for 2% of the time, Pallas kernels for 12%

profile of v1, /device:TPU:1, one launch (start us, length us, event | category | flops | bytes accessed | tf_op | source)
XLA Modules:
  0.0 223.3 jit_solution(3648226424598666687)
XLA Ops:
  0.9 1.5 select_maximum_fusion.refs_0_
  2.4 2.2 collective-permute-start.18
  5.8 1.5 collective-permute-start.12
  7.2 1.6 collective-permute-start
  8.9 1.8 collective-permute-start.9
  10.7 27.7 %collective-permute-done.18.refs_15_.refs_17_.refs_19_ = f32[3080,128]{1,0:T(8,128)S(1)} collective-permute-done((f32[3080,128]{1,0:T(8,128)S(1)}, f32[3080,128]{1,0:T(8,128)S(1)}, u32[]{:S(2)}, u32[]{:S(2)}) %collective-permute-start.18) | collective-permute-done | bytes 1576992 | tf_op jit(solution)/shard_map/ppermute | solution.py:41
  38.4 3.1 %collective-permute-start.4 = (f32[3080,128]{1,0:T(8,128)S(1)}, f32[3080,128]{1,0:T(8,128)S(1)}, u32[]{:S(2)}, u32[]{:S(2)}) collective-permute-start(f32[3080,128]{1,0:T(8,128)S(1)} %select_maximum_fusion.refs_0_), channel_id=1, source_target_pairs={{0,8},{1,9},{2,10},{3,11},{4,12},{5,13},{6,14},{7,15},{64,72},{65,... | collective-permute-start | bytes 4730888 | tf_op jit(solution)/shard_map/ppermute | solution.py:41
  41.6 3.8 %collective-permute-start.1 = (f32[3080,128]{1,0:T(8,128)S(1)}, f32[3080,128]{1,0:T(8,128)S(1)}, u32[]{:S(2)}, u32[]{:S(2)}) collective-permute-start(f32[3080,128]{1,0:T(8,128)S(1)} %select_maximum_fusion.refs_0_), channel_id=1, source_target_pairs={{0,6},{1,7},{2,0},{3,1},{4,2},{5,3},{6,4},{7,5},{64,70},{65,71},{6... | collective-permute-start | bytes 4730888 | tf_op jit(solution)/shard_map/ppermute | solution.py:41
  46.7 1.5 collective-permute-start.22
  49.5 25.3 %collective-permute-done.4.refs_5_ = f32[3080,128]{1,0:T(8,128)S(1)} collective-permute-done((f32[3080,128]{1,0:T(8,128)S(1)}, f32[3080,128]{1,0:T(8,128)S(1)}, u32[]{:S(2)}, u32[]{:S(2)}) %collective-permute-start.4) | collective-permute-done | bytes 1576992 | tf_op jit(solution)/shard_map/ppermute | solution.py:41
  74.7 2.4 %collective-permute-start.15 = (f32[1544,128]{1,0:T(8,128)S(1)}, f32[1544,128]{1,0:T(8,128)S(1)}, u32[]{:S(2)}, u32[]{:S(2)}) collective-permute-start(f32[1544,128]{1,0:T(8,128)S(1)} %slice.37), channel_id=1, source_target_pairs={{0,48},{1,49},{2,50},{3,51},{4,52},{5,53},{6,54},{7,55},{64,112},{... | collective-permute-start | bytes 2371592 | tf_op jit(solution)/shard_map/ppermute | solution.py:41
  78.6 3.5 %collective-permute-start.3 = (f32[1544,128]{1,0:T(8,128)S(1)}, f32[1544,128]{1,0:T(8,128)S(1)}, u32[]{:S(2)}, u32[]{:S(2)}) collective-permute-start(f32[1544,128]{1,0:T(8,128)S(1)} %slice.33), channel_id=1, source_target_pairs={{0,6},{1,7},{2,0},{3,1},{4,2},{5,3},{6,4},{7,5},{64,70},{65,71},{6... | collective-permute-start | bytes 2371592 | tf_op jit(solution)/shard_map/ppermute | solution.py:41
  83.0 3.2 %collective-permute-start.16 = (f32[1536,128]{1,0:T(8,128)S(1)}, f32[1536,128]{1,0:T(8,128)S(1)}, u32[]{:S(2)}, u32[]{:S(2)}) collective-permute-start(f32[1536,128]{1,0:T(8,128)S(1)} %collective-permute-done.14.refs_11_.refs_13_.refs_15_), channel_id=1, source_target_pairs={{0,1},{1,0},{2,3},{3,2},{4,5},{5,4},{6,7},{7,6},{64,65},{65,64},{6... | collective-permute-start | bytes 2359304 | tf_op jit(solution)/shard_map/ppermute | solution.py:41
  87.2 10.2 %collective-permute-done.15.refs_12_.refs_14_.refs_16_ = f32[1544,128]{1,0:T(8,128)S(1)} collective-permute-done((f32[1544,128]{1,0:T(8,128)S(1)}, f32[1544,128]{1,0:T(8,128)S(1)}, u32[]{:S(2)}, u32[]{:S(2)}) %collective-permute-start.15) | collective-permute-done | bytes 790560 | tf_op jit(solution)/shard_map/ppermute | solution.py:41
  97.4 3.1 %collective-permute-start.19 = (f32[3080,128]{1,0:T(8,128)S(1)}, f32[3080,128]{1,0:T(8,128)S(1)}, u32[]{:S(2)}, u32[]{:S(2)}) collective-permute-start(f32[3080,128]{1,0:T(8,128)S(1)} %collective-permute-done.18.refs_15_.refs_17_.refs_19_), channel_id=1, source_target_pairs={{0,1},{1,0},{2,3},{3,2},{4,5},{5,4},{6,7},{7,6},{64,65},{65,64},{6... | collective-permute-start | bytes 4730888 | tf_op jit(solution)/shard_map/ppermute | solution.py:41
  105.2 6.9 %collective-permute-done.20.refs_19_.refs_21_ = f32[3080,128]{1,0:T(8,128)} collective-permute-done((f32[3080,128]{1,0:T(8,128)S(1)}, f32[3080,128]{1,0:T(8,128)}, u32[]{:S(2)}, u32[]{:S(2)}) %collective-permute-start.20) | collective-permute-done | bytes 1576992 | tf_op jit(solution)/shard_map/ppermute | solution.py:41
  112.0 1.4 collective-permute-start.5
  114.6 3.8 %collective-permute-start.23 = (f32[3080,128]{1,0:T(8,128)S(1)}, f32[3080,128]{1,0:T(8,128)S(1)}, u32[]{:S(2)}, u32[]{:S(2)}) collective-permute-start(f32[3080,128]{1,0:T(8,128)S(1)} %collective-permute-done.22.refs_21_.refs_23_), channel_id=1, source_target_pairs={{0,1},{1,0},{2,3},{3,2},{4,5},{5,4},{6,7},{7,6},{64,65},{65,64},{6... | collective-permute-start | bytes 4730888 | tf_op jit(solution)/shard_map/ppermute | solution.py:41
  121.4 18.6 %collective-permute-done.6.refs_7_ = f32[3080,128]{1,0:T(8,128)S(1)} collective-permute-done((f32[3080,128]{1,0:T(8,128)S(1)}, f32[3080,128]{1,0:T(8,128)S(1)}, u32[]{:S(2)}, u32[]{:S(2)}) %collective-permute-start.6) | collective-permute-done | bytes 1576992 | tf_op jit(solution)/shard_map/ppermute | solution.py:41
  140.0 2.7 %collective-permute-start.25 = (f32[1544,128]{1,0:T(8,128)S(1)}, f32[1544,128]{1,0:T(8,128)}, u32[]{:S(2)}, u32[]{:S(2)}) collective-permute-start(f32[1544,128]{1,0:T(8,128)S(1)} %slice.39), channel_id=1, source_target_pairs={{0,48},{1,49},{2,50},{3,51},{4,52},{5,53},{6,54},{7,55},{64,112},{... | collective-permute-start | bytes 2371592 | tf_op jit(solution)/shard_map/ppermute | solution.py:41
  143.9 3.0 %collective-permute-done.5.refs_6_ = f32[3080,128]{1,0:T(8,128)S(1)} collective-permute-done((f32[3080,128]{1,0:T(8,128)S(1)}, f32[3080,128]{1,0:T(8,128)S(1)}, u32[]{:S(2)}, u32[]{:S(2)}) %collective-permute-start.5) | collective-permute-done | bytes 1576992 | tf_op jit(solution)/shard_map/ppermute | solution.py:41
  150.4 8.4 %collective-permute-done.25.refs_26_ = f32[1544,128]{1,0:T(8,128)} collective-permute-done((f32[1544,128]{1,0:T(8,128)S(1)}, f32[1544,128]{1,0:T(8,128)}, u32[]{:S(2)}, u32[]{:S(2)}) %collective-permute-start.25) | collective-permute-done | bytes 790560 | tf_op jit(solution)/shard_map/ppermute | solution.py:41
  158.8 1.7 collective-permute-start.27
  164.4 5.0 %collective-permute-start.26 = (f32[1536,128]{1,0:T(8,128)}, f32[1536,128]{1,0:T(8,128)}, u32[]{:S(2)}, u32[]{:S(2)}) collective-permute-start(f32[1536,128]{1,0:T(8,128)} %collective-permute-done.24.refs_25_), channel_id=1, source_target_pairs={{0,1},{1,0},{2,3},{3,2},{4,5},{5,4},{6,7},{7,6},{64,65},{65,64},{6... | collective-permute-start | bytes 2359304 | tf_op jit(solution)/shard_map/ppermute | solution.py:41
  173.4 1.4 copy-done.1
  174.8 1.4 copy-done.3
  176.2 1.4 copy-done.5
  177.6 1.4 copy-done.7
  179.0 1.4 copy-done.9
  193.5 16.2 %shard_map.48.refs_23_ = f32[3072,128]{1,0:T(8,128)S(1)} custom-call(s32[1]{0:T(128)} %bitcast.depth_ref, s32[3,17]{1,0:T(4,128)S(1)} %copy-done.38, s32[6,4]{1,0:T(8,128)S(1)} %copy.12.kept_ref, f32[3080,128]{1,0:T(8,128)S(1)} %select_maximum_fusion.refs_0_, f32[3080,128]{1,0:T(8,128)S(1)} %copy-done.5, f32[3080,128]{1,0:T(8,128)S(1)} %copy-done.1, ...), custom_call_target="tpu_custom_call" | custom-call | flops 1200000000 | bytes 15000000 | tf_op jit(solution)/shard_map/pallas_call | solution.py:231
  209.8 7.7 %shard_map.49.refs_29_ = f32[3072,128]{1,0:T(8,128)S(1)} custom-call(s32[1]{0:T(128)} %bitcast.depth_ref, s32[3,17]{1,0:T(4,128)S(1)} %copy-done.38, s32[6,4]{1,0:T(8,128)S(1)} %copy.12.kept_ref, f32[3080,128]{1,0:T(8,128)S(1)} %select_maximum_fusion.refs_0_, f32[3080,128]{1,0:T(8,128)S(1)} %copy-done.5, f32[3080,128]{1,0:T(8,128)S(1)} %copy-done.1, ...), custom_call_target="tpu_custom_call" | custom-call | flops 1200000000 | bytes 15000000 | tf_op jit(solution)/shard_map/pallas_call | solution.py:231
  217.5 5.6 %shard_map.50 = f32[3072,128]{1,0:T(8,128)} custom-call(s32[1]{0:T(128)} %bitcast.depth_ref, s32[3,17]{1,0:T(4,128)S(1)} %copy-done.38, s32[6,4]{1,0:T(8,128)S(1)} %copy.12.kept_ref, f32[3080,128]{1,0:T(8,128)S(1)} %select_maximum_fusion.refs_0_, f32[3080,128]{1,0:T(8,128)S(1)} %copy-done.5, f32[3080,128]{1,0:T(8,128)S(1)} %copy-done.1, ...), custom_call_target="tpu_custom_call" | custom-call | flops 800000000 | bytes 10000000 | tf_op jit(solution)/shard_map/pallas_call | solution.py:231
  (123 shorter events, 42.4 us)
Async XLA Ops:
  2.4 36.0 %collective-permute-start.18 = (f32[3080,128]{1,0:T(8,128)S(1)}, f32[3080,128]{1,0:T(8,128)S(1)}, u32[]{:S(2)}, u32[]{:S(2)}) collective-permute-start(f32[3080,128]{1,0:T(8,128)S(1)} %select_maximum_fusion.refs_0_), channel_id=1, source_target_pairs={{0,64},{1,65},{2,66},{3,67},{4,68},{5,69},{6,70},{7,71},{64,0},{65... | collective-permute-start | bytes 4730888 | tf_op jit(solution)/shard_map/ppermute | solution.py:41
  4.6 37.0 %collective-permute-start.10 = (f32[3080,128]{1,0:T(8,128)S(1)}, f32[3080,128]{1,0:T(8,128)S(1)}, u32[]{:S(2)}, u32[]{:S(2)}) collective-permute-start(f32[3080,128]{1,0:T(8,128)S(1)} %select_maximum_fusion.refs_0_), channel_id=1, source_target_pairs={{0,16},{1,17},{2,18},{3,19},{4,20},{5,21},{6,22},{7,23},{64,80},{6... | collective-permute-start | bytes 4730888 | tf_op jit(solution)/shard_map/ppermute | solution.py:41
  5.8 39.6 %collective-permute-start.12 = (f32[3080,128]{1,0:T(8,128)S(1)}, f32[3080,128]{1,0:T(8,128)S(1)}, u32[]{:S(2)}, u32[]{:S(2)}) collective-permute-start(f32[3080,128]{1,0:T(8,128)S(1)} %select_maximum_fusion.refs_0_), channel_id=1, source_target_pairs={{0,48},{1,49},{2,50},{3,51},{4,52},{5,53},{6,54},{7,55},{64,112},{... | collective-permute-start | bytes 4730888 | tf_op jit(solution)/shard_map/ppermute | solution.py:41
  7.2 39.4 %collective-permute-start = (f32[3080,128]{1,0:T(8,128)S(1)}, f32[3080,128]{1,0:T(8,128)S(1)}, u32[]{:S(2)}, u32[]{:S(2)}) collective-permute-start(f32[3080,128]{1,0:T(8,128)S(1)} %select_maximum_fusion.refs_0_), channel_id=1, source_target_pairs={{0,2},{1,3},{2,4},{3,5},{4,6},{5,7},{6,0},{7,1},{64,66},{65,67},{6... | collective-permute-start | bytes 4730888 | tf_op jit(solution)/shard_map/ppermute | solution.py:41
  8.9 39.4 %collective-permute-start.9 = (f32[3080,128]{1,0:T(8,128)S(1)}, f32[3080,128]{1,0:T(8,128)S(1)}, u32[]{:S(2)}, u32[]{:S(2)}) collective-permute-start(f32[3080,128]{1,0:T(8,128)S(1)} %select_maximum_fusion.refs_0_), channel_id=1, source_target_pairs={{0,1},{1,0},{2,3},{3,2},{4,5},{5,4},{6,7},{7,6},{64,65},{65,64},{6... | collective-permute-start | bytes 4730888 | tf_op jit(solution)/shard_map/ppermute | solution.py:41
  38.4 36.3 %collective-permute-start.4 = (f32[3080,128]{1,0:T(8,128)S(1)}, f32[3080,128]{1,0:T(8,128)S(1)}, u32[]{:S(2)}, u32[]{:S(2)}) collective-permute-start(f32[3080,128]{1,0:T(8,128)S(1)} %select_maximum_fusion.refs_0_), channel_id=1, source_target_pairs={{0,8},{1,9},{2,10},{3,11},{4,12},{5,13},{6,14},{7,15},{64,72},{65,... | collective-permute-start | bytes 4730888 | tf_op jit(solution)/shard_map/ppermute | solution.py:41
  41.6 61.0 %copy-start.2 = (f32[3080,128]{1,0:T(8,128)}, f32[3080,128]{1,0:T(8,128)S(1)}, u32[]{:S(2)}) copy-start(f32[3080,128]{1,0:T(8,128)S(1)} %collective-permute-done.10.refs_7_.refs_9_.refs_11_) | copy-start | bytes 4730884
  41.6 35.8 %collective-permute-start.1 = (f32[3080,128]{1,0:T(8,128)S(1)}, f32[3080,128]{1,0:T(8,128)S(1)}, u32[]{:S(2)}, u32[]{:S(2)}) collective-permute-start(f32[3080,128]{1,0:T(8,128)S(1)} %select_maximum_fusion.refs_0_), channel_id=1, source_target_pairs={{0,6},{1,7},{2,0},{3,1},{4,2},{5,3},{6,4},{7,5},{64,70},{65,71},{6... | collective-permute-start | bytes 4730888 | tf_op jit(solution)/shard_map/ppermute | solution.py:41
  45.4 33.2 %collective-permute-start.14 = (f32[1536,128]{1,0:T(8,128)S(1)}, f32[1536,128]{1,0:T(8,128)S(1)}, u32[]{:S(2)}, u32[]{:S(2)}) collective-permute-start(f32[1536,128]{1,0:T(8,128)S(1)} %slice.36), channel_id=1, source_target_pairs={{0,16},{1,17},{2,18},{3,19},{4,20},{5,21},{6,22},{7,23},{64,80},{6... | collective-permute-start | bytes 2359304 | tf_op jit(solution)/shard_map/ppermute | solution.py:41
  46.7 57.3 %collective-permute-start.22 = (f32[3080,128]{1,0:T(8,128)S(1)}, f32[3080,128]{1,0:T(8,128)S(1)}, u32[]{:S(2)}, u32[]{:S(2)}) collective-permute-start(f32[3080,128]{1,0:T(8,128)S(1)} %collective-permute-done.18.refs_15_.refs_17_.refs_19_), channel_id=1, source_target_pairs={{0,48},{1,49},{2,50},{3,51},{4,52},{5,53},{6,54},{7,55},{64,112},{... | collective-permute-start | bytes 4730888 | tf_op jit(solution)/shard_map/ppermute | solution.py:41
  49.5 32.7 %collective-permute-start.2 = (f32[1536,128]{1,0:T(8,128)S(1)}, f32[1536,128]{1,0:T(8,128)S(1)}, u32[]{:S(2)}, u32[]{:S(2)}) collective-permute-start(f32[1536,128]{1,0:T(8,128)S(1)} %slice.32), channel_id=1, source_target_pairs={{0,2},{1,3},{2,4},{3,5},{4,6},{5,7},{6,0},{7,1},{64,66},{65,67},{6... | collective-permute-start | bytes 2359304 | tf_op jit(solution)/shard_map/ppermute | solution.py:41
  74.7 22.7 %collective-permute-start.15 = (f32[1544,128]{1,0:T(8,128)S(1)}, f32[1544,128]{1,0:T(8,128)S(1)}, u32[]{:S(2)}, u32[]{:S(2)}) collective-permute-start(f32[1544,128]{1,0:T(8,128)S(1)} %slice.37), channel_id=1, source_target_pairs={{0,48},{1,49},{2,50},{3,51},{4,52},{5,53},{6,54},{7,55},{64,112},{... | collective-permute-start | bytes 2371592 | tf_op jit(solution)/shard_map/ppermute | solution.py:41
  77.4 41.2 %copy-start = (f32[3080,128]{1,0:T(8,128)}, f32[3080,128]{1,0:T(8,128)S(1)}, u32[]{:S(2)}) copy-start(f32[3080,128]{1,0:T(8,128)S(1)} %collective-permute-done.1.refs_2_) | copy-start | bytes 4730884
  77.4 34.7 %collective-permute-start.20 = (f32[3080,128]{1,0:T(8,128)S(1)}, f32[3080,128]{1,0:T(8,128)}, u32[]{:S(2)}, u32[]{:S(2)}) collective-permute-start(f32[3080,128]{1,0:T(8,128)S(1)} %collective-permute-done.18.refs_15_.refs_17_.refs_19_), channel_id=1, source_target_pairs={{0,16},{1,17},{2,18},{3,19},{4,20},{5,21},{6,22},{7,23},{64,80},{6... | collective-permute-start | bytes 4730888 | tf_op jit(solution)/shard_map/ppermute | solution.py:41
  78.6 23.0 %collective-permute-start.3 = (f32[1544,128]{1,0:T(8,128)S(1)}, f32[1544,128]{1,0:T(8,128)S(1)}, u32[]{:S(2)}, u32[]{:S(2)}) collective-permute-start(f32[1544,128]{1,0:T(8,128)S(1)} %slice.33), channel_id=1, source_target_pairs={{0,6},{1,7},{2,0},{3,1},{4,2},{5,3},{6,4},{7,5},{64,70},{65,71},{6... | collective-permute-start | bytes 2371592 | tf_op jit(solution)/shard_map/ppermute | solution.py:41
  83.0 19.5 %collective-permute-start.16 = (f32[1536,128]{1,0:T(8,128)S(1)}, f32[1536,128]{1,0:T(8,128)S(1)}, u32[]{:S(2)}, u32[]{:S(2)}) collective-permute-start(f32[1536,128]{1,0:T(8,128)S(1)} %collective-permute-done.14.refs_11_.refs_13_.refs_15_), channel_id=1, source_target_pairs={{0,1},{1,0},{2,3},{3,2},{4,5},{5,4},{6,7},{7,6},{64,65},{65,64},{6... | collective-permute-start | bytes 2359304 | tf_op jit(solution)/shard_map/ppermute | solution.py:41
  97.4 17.2 %collective-permute-start.19 = (f32[3080,128]{1,0:T(8,128)S(1)}, f32[3080,128]{1,0:T(8,128)S(1)}, u32[]{:S(2)}, u32[]{:S(2)}) collective-permute-start(f32[3080,128]{1,0:T(8,128)S(1)} %collective-permute-done.18.refs_15_.refs_17_.refs_19_), channel_id=1, source_target_pairs={{0,1},{1,0},{2,3},{3,2},{4,5},{5,4},{6,7},{7,6},{64,65},{65,64},{6... | collective-permute-start | bytes 4730888 | tf_op jit(solution)/shard_map/ppermute | solution.py:41
  102.6 15.9 %collective-permute-start.13 = (f32[3080,128]{1,0:T(8,128)S(1)}, f32[3080,128]{1,0:T(8,128)S(1)}, u32[]{:S(2)}, u32[]{:S(2)}) collective-permute-start(f32[3080,128]{1,0:T(8,128)S(1)} %collective-permute-done.12.refs_9_.refs_11_.refs_13_), channel_id=1, source_target_pairs={{0,1},{1,0},{2,3},{3,2},{4,5},{5,4},{6,7},{7,6},{64,65},{65,64},{6... | collective-permute-start | bytes 4730888 | tf_op jit(solution)/shard_map/ppermute | solution.py:41
  103.5 16.4 %collective-permute-start.11 = (f32[3080,128]{1,0:T(8,128)S(1)}, f32[3080,128]{1,0:T(8,128)S(1)}, u32[]{:S(2)}, u32[]{:S(2)}) collective-permute-start(f32[3080,128]{1,0:T(8,128)S(1)} %collective-permute-done.10.refs_7_.refs_9_.refs_11_), channel_id=1, source_target_pairs={{0,1},{1,0},{2,3},{3,2},{4,5},{5,4},{6,7},{7,6},{64,65},{65,64},{6... | collective-permute-start | bytes 4730888 | tf_op jit(solution)/shard_map/ppermute | solution.py:41
  104.0 36.0 %collective-permute-start.6 = (f32[3080,128]{1,0:T(8,128)S(1)}, f32[3080,128]{1,0:T(8,128)S(1)}, u32[]{:S(2)}, u32[]{:S(2)}) collective-permute-start(f32[3080,128]{1,0:T(8,128)S(1)} %collective-permute-done.4.refs_5_), channel_id=1, source_target_pairs={{0,6},{1,7},{2,0},{3,1},{4,2},{5,3},{6,4},{7,5},{64,70},{65,71},{6... | collective-permute-start | bytes 4730888 | tf_op jit(solution)/shard_map/ppermute | solution.py:41
  112.0 34.9 %collective-permute-start.5 = (f32[3080,128]{1,0:T(8,128)S(1)}, f32[3080,128]{1,0:T(8,128)S(1)}, u32[]{:S(2)}, u32[]{:S(2)}) collective-permute-start(f32[3080,128]{1,0:T(8,128)S(1)} %collective-permute-done.4.refs_5_), channel_id=1, source_target_pairs={{0,2},{1,3},{2,4},{3,5},{4,6},{5,7},{6,0},{7,1},{64,66},{65,67},{6... | collective-permute-start | bytes 4730888 | tf_op jit(solution)/shard_map/ppermute | solution.py:41
  114.6 29.3 %copy-start.12 = (f32[3080,128]{1,0:T(8,128)}, f32[3080,128]{1,0:T(8,128)S(1)}, u32[]{:S(2)}) copy-start(f32[3080,128]{1,0:T(8,128)S(1)} %collective-permute-done.19.refs_16_.refs_18_.refs_20_) | copy-start | bytes 4730884
  114.6 48.6 %collective-permute-start.23 = (f32[3080,128]{1,0:T(8,128)S(1)}, f32[3080,128]{1,0:T(8,128)S(1)}, u32[]{:S(2)}, u32[]{:S(2)}) collective-permute-start(f32[3080,128]{1,0:T(8,128)S(1)} %collective-permute-done.22.refs_21_.refs_23_), channel_id=1, source_target_pairs={{0,1},{1,0},{2,3},{3,2},{4,5},{5,4},{6,7},{7,6},{64,65},{65,64},{6... | collective-permute-start | bytes 4730888 | tf_op jit(solution)/shard_map/ppermute | solution.py:41
  118.4 91.3 %collective-permute-start.21 = (f32[3080,128]{1,0:T(8,128)}, f32[3080,128]{1,0:T(8,128)}, u32[]{:S(2)}, u32[]{:S(2)}) collective-permute-start(f32[3080,128]{1,0:T(8,128)} %collective-permute-done.20.refs_19_.refs_21_), channel_id=1, source_target_pairs={{0,1},{1,0},{2,3},{3,2},{4,5},{5,4},{6,7},{7,6},{64,65},{65,64},{6... | collective-permute-start | bytes 4730888 | tf_op jit(solution)/shard_map/ppermute | solution.py:41
  119.9 29.2 %collective-permute-start.17 = (f32[1544,128]{1,0:T(8,128)S(1)}, f32[1544,128]{1,0:T(8,128)S(1)}, u32[]{:S(2)}, u32[]{:S(2)}) collective-permute-start(f32[1544,128]{1,0:T(8,128)S(1)} %collective-permute-done.15.refs_12_.refs_14_.refs_16_), channel_id=1, source_target_pairs={{0,1},{1,0},{2,3},{3,2},{4,5},{5,4},{6,7},{7,6},{64,65},{65,64},{6... | collective-permute-start | bytes 2371592 | tf_op jit(solution)/shard_map/ppermute | solution.py:41
  140.0 18.8 %collective-permute-start.25 = (f32[1544,128]{1,0:T(8,128)S(1)}, f32[1544,128]{1,0:T(8,128)}, u32[]{:S(2)}, u32[]{:S(2)}) collective-permute-start(f32[1544,128]{1,0:T(8,128)S(1)} %slice.39), channel_id=1, source_target_pairs={{0,48},{1,49},{2,50},{3,51},{4,52},{5,53},{6,54},{7,55},{64,112},{... | collective-permute-start | bytes 2371592 | tf_op jit(solution)/shard_map/ppermute | solution.py:41
  143.9 29.3 %copy-start.39 = (s32[6,4]{0,1:T(4,128)S(1)}, s32[6,4]{0,1:T(4,128)}, u32[]{:S(2)}) copy-start(s32[6,4]{0,1:T(4,128)} %param.6) | copy-start | bytes 292
  146.9 16.3 %collective-permute-start.24 = (f32[1536,128]{1,0:T(8,128)S(1)}, f32[1536,128]{1,0:T(8,128)}, u32[]{:S(2)}, u32[]{:S(2)}) collective-permute-start(f32[1536,128]{1,0:T(8,128)S(1)} %slice.38), channel_id=1, source_target_pairs={{0,16},{1,17},{2,18},{3,19},{4,20},{5,21},{6,22},{7,23},{64,80},{6... | collective-permute-start | bytes 2359304 | tf_op jit(solution)/shard_map/ppermute | solution.py:41
  149.1 68.4 %collective-permute-start.8 = (f32[1544,128]{1,0:T(8,128)}, f32[1544,128]{1,0:T(8,128)}, u32[]{:S(2)}, u32[]{:S(2)}) collective-permute-start(f32[1544,128]{1,0:T(8,128)} %slice.35), channel_id=1, source_target_pairs={{0,6},{1,7},{2,0},{3,1},{4,2},{5,3},{6,4},{7,5},{64,70},{65,71},{6... | collective-permute-start | bytes 2371592 | tf_op jit(solution)/shard_map/ppermute | solution.py:41
  158.8 58.7 %collective-permute-start.27 = (f32[1544,128]{1,0:T(8,128)}, f32[1544,128]{1,0:T(8,128)}, u32[]{:S(2)}, u32[]{:S(2)}) collective-permute-start(f32[1544,128]{1,0:T(8,128)} %collective-permute-done.25.refs_26_), channel_id=1, source_target_pairs={{0,1},{1,0},{2,3},{3,2},{4,5},{5,4},{6,7},{7,6},{64,65},{65,64},{6... | collective-permute-start | bytes 2371592 | tf_op jit(solution)/shard_map/ppermute | solution.py:41
  163.2 54.2 %collective-permute-start.7 = (f32[1536,128]{1,0:T(8,128)}, f32[1536,128]{1,0:T(8,128)}, u32[]{:S(2)}, u32[]{:S(2)}) collective-permute-start(f32[1536,128]{1,0:T(8,128)} %slice.34), channel_id=1, source_target_pairs={{0,2},{1,3},{2,4},{3,5},{4,6},{5,7},{6,0},{7,1},{64,66},{65,67},{6... | collective-permute-start | bytes 2359304 | tf_op jit(solution)/shard_map/ppermute | solution.py:41
  164.4 53.1 %collective-permute-start.26 = (f32[1536,128]{1,0:T(8,128)}, f32[1536,128]{1,0:T(8,128)}, u32[]{:S(2)}, u32[]{:S(2)}) collective-permute-start(f32[1536,128]{1,0:T(8,128)} %collective-permute-done.24.refs_25_), channel_id=1, source_target_pairs={{0,1},{1,0},{2,3},{3,2},{4,5},{5,4},{6,7},{7,6},{64,65},{65,64},{6... | collective-permute-start | bytes 2359304 | tf_op jit(solution)/shard_map/ppermute | solution.py:41
  (36 other events, 167.1 us)

commit v2 on v1

v2 whole, which is shorter than its diff:
```python
import functools

import jax
import jax.numpy as jnp
import numpy as np
from jax import lax
from jax.experimental import pallas as pl
from jax.experimental.pallas import tpu as pltpu
from jax.sharding import PartitionSpec as P


AXES = ("row", "col", "depth")
RING = 4
HALF = 6
SLOTS = 4
BS = 128
ROWS = HALF * SLOTS * BS
EXTRA = 8
GROUP = 8
CUT = ROWS // 2
THIRD = ROWS // 3
TRASH = HALF * SLOTS
F32, BF16 = jnp.float32, jnp.bfloat16


def device_number(x, y, z, d):
    y_hi, y_lo = y >> 1, y & 1
    return (y_lo * RING + x) * 16 + (y_hi * RING + z) * 2 + d


def all_places():
    return [(x, y, z, d) for x in range(4) for y in range(4) for z in range(4) for d in range(2)]


def move(value, dx=0, dz=0, y_flip=0, d_flip=0):
    pairs = [
        (
            device_number(x, y, z, d),
            device_number(
                (x + dx * (1 - 2 * d)) % 4, y ^ y_flip, (z + dz * (1 - 2 * d)) % 4, d ^ d_flip
            ),
        )
        for x, y, z, d in all_places()
    ]
    return lax.ppermute(value, AXES, pairs)


LEFT_STAGE = (0, 0, 1, 2, 1, 2, 6, 7)
RIGHT_STAGE = (0, 0, 1, 2, 3, 4, 8, 4, 8, 5)
STAGES = 9
WIDTH = 18


def panel_table():
    table = np.zeros((128, STAGES, WIDTH), np.int32)
    for x, y, z, d in all_places():
        rows = table[device_number(x, y, z, d)]
        rows[:, WIDTH - 1] = d
        place = (0, 1, 3, 2) if d else (0, 2, 3, 1)
        for h in range(2):
            for w in range(4):
                left = 4 * (h != y >> 1) + place[(w - z) % 4]
                right = place[(w - x) % 4]
                for source in [(right,), ((4,), (5, 6), (7, 8), (9,))[right]][h != (y & 1)]:
                    row = rows[max(LEFT_STAGE[left], RIGHT_STAGE[source])]
                    row[1 + 2 * row[0]] = left
                    row[2 + 2 * row[0]] = source
                    row[0] += 1
    return table


def split(value):
    high = value.astype(BF16)
    return high, (value - high.astype(F32)).astype(BF16)


def product(a, b):
    a_high, a_low = split(a)
    b_high, b_low = split(b)
    side = jnp.concatenate([b_high, b_low], 1)
    both = jnp.dot(
        jnp.concatenate([a_high, a_low], 1),
        jnp.concatenate([side, side], 0),
        preferred_element_type=F32,
    )
    return both[:, :BS] + both[:, BS:]


def table_kernel(meta_ref, kept_ref, o_ref):
    for i in range(STAGES):
        for j in range(WIDTH):
            o_ref[i, j] = meta_ref[i, j]
    for i in range(HALF):
        for u in range(SLOTS):
            o_ref[STAGES + i, u] = kept_ref[i, u]


def gate_kernel(a_ref, o_ref):
    for i in range(STAGES):
        for j in range(WIDTH):
            o_ref[i, j] = a_ref[i, j]
    for i in range(HALF):
        for u in range(SLOTS):
            o_ref[STAGES + i, u] = a_ref[STAGES + i, u]


def gate(body, *args):
    return pl.pallas_call(
        body,
        out_shape=jax.ShapeDtypeStruct((STAGES + HALF, WIDTH), jnp.int32),
        in_specs=[pl.BlockSpec(memory_space=pltpu.SMEM)] * len(args),
        out_specs=pl.BlockSpec(memory_space=pltpu.SMEM),
        cost_estimate=pl.CostEstimate(flops=100, bytes_accessed=1000, transcendentals=0),
    )(*args)


def panels_kernel(stage, lefts, rights, n_refs, meta_ref, *refs):
    first, last = stage == 0, stage == STAGES - 1
    pieces = refs[:n_refs]
    at = n_refs if first else n_refs + 1
    out, lb, rb, lc, rc, inv, lst, sem, csem = refs[at : at + 9]
    cb = refs[at + 9] if last else out
    depth = meta_ref[0, WIDTH - 1]
    count = meta_ref[stage, 0]
    whole = pl.ds(0, ROWS)

    def copies(j, sources, dst, cols, data_sem, col_sem):
        for ref, src, rows, to, has_cols in sources[j]:
            pltpu.make_async_copy(
                pieces[ref].at[pl.ds(src, rows)], dst.at[pl.ds(to, rows)], data_sem
            ).start()
            if has_cols:
                pltpu.make_async_copy(
                    pieces[ref].at[pl.ds(src + rows, EXTRA)], cols, col_sem
                ).start()

    def fetch(n, slot):
        left, right = meta_ref[stage, 1 + 2 * n], meta_ref[stage, 2 + 2 * n]
        for j in lefts:
            @pl.when(left == j)
            def _():
                copies(j, lefts, lb.at[slot], lc.at[slot], sem.at[slot, 0], csem.at[slot, 0])
        for j in rights:
            @pl.when(right == j)
            def _():
                for mine in range(2):
                    half = depth if mine == 0 else 1 - depth
                    copies(
                        (j, mine),
                        rights[j],
                        rb.at[slot, pl.ds(pl.multiple_of(half * ROWS, ROWS), ROWS)],
                        rc.at[slot, half],
                        sem.at[slot, 1 + mine],
                        csem.at[slot, 1 + mine],
                    )

    @pl.when(count > 0)
    def _():
        fetch(0, 0)

    if first:
        cb[...] = jnp.zeros_like(cb)
    else:
        cb[...] = refs[n_refs][...]

    @pl.when(count > 0)
    def _():
        def clear(n, carry):
            inv[n] = -1
            return carry

        lax.fori_loop(0, HALF * 16, clear, 0)
        for i in range(HALF):
            for u in range(SLOTS):
                inv[i * 16 + meta_ref[STAGES + i, u]] = u

    def panel(n, carry):
        slot = lax.rem(n, 2)
        source = meta_ref[stage, 2 + 2 * n]
        part = jnp.where(jnp.logical_or(source < 5, source > 8), 2, (source + 1) & 1)
        low = jnp.where(part == 1, HALF // 2, 0)
        high = jnp.where(part == 0, HALF // 2, HALF)

        @pl.when(n + 1 < count)
        def _():
            fetch(n + 1, 1 - slot)

        pltpu.make_async_copy(lc.at[slot], lc.at[slot], csem.at[slot, 0]).wait()
        for mine in range(2):
            pltpu.make_async_copy(rc.at[slot, 0], rc.at[slot, 0], csem.at[slot, 1 + mine]).wait()

        def list_row(e, total):
            i = e // SLOTS
            k = lc[slot, 0, e].astype(jnp.int32)
            half = (k >= HALF).astype(jnp.int32)
            within = k - HALF * half
            there = jnp.logical_and(within >= low, within < high).astype(jnp.int32)
            base = within * SLOTS
            code = e + k * 256
            for t in range(SLOTS):
                column = rc[slot, half, 0, base + t].astype(jnp.int32)
                u = inv[i * 16 + column]
                lst[total] = code + t * 64 + (i * SLOTS + u) * 4096
                total = total + jnp.where(u >= 0, there, 0)
            return total

        total = lax.fori_loop(0, HALF * SLOTS, list_row, 0)
        for q in range(GROUP):
            lst[total + q] = TRASH * 4096
        pltpu.make_async_copy(lb.at[slot], lb.at[slot], sem.at[slot, 0]).wait()
        for rows, when in ((ROWS, part == 2), (CUT, part < 2)):
            @pl.when(when)
            def _():
                for mine in range(2):
                    view = rb.at[slot, pl.ds(0, rows)]
                    pltpu.make_async_copy(view, view, sem.at[slot, 1 + mine]).wait()

        def group(g, carry):
            done = []
            for q in range(GROUP):
                code = lst[g * GROUP + q]
                a = pl.multiple_of((code & 63) * BS, BS)
                b = pl.multiple_of(((code >> 6) & 63) * BS, BS)
                c = pl.multiple_of((code >> 12) * BS, BS)
                done.append((c, product(lb[slot, pl.ds(a, BS)], rb[slot, pl.ds(b, BS)])))
            for c, value in done:
                cb[pl.ds(c, BS)] += value
            return carry

        lax.fori_loop(0, (total + GROUP - 1) // GROUP, group, 0)
        return carry

    lax.fori_loop(0, count, panel, 0)
    if last:
        store = pltpu.make_async_copy(cb.at[whole], out, sem.at[0, 3])
        store.start()
        store.wait()


def add_panels(stage, lefts, rights, before, meta, panels):
    arrays, numbers = [], {}

    def numbered(pieces):
        out = []
        for array, *rest in pieces:
            if id(array) not in numbers:
                numbers[id(array)] = len(arrays)
                arrays.append(array)
            out.append((numbers[id(array)], *rest))
        return out

    left_refs = {j: numbered(p) for j, p in lefts.items()}
    right_refs = {j: {k: numbered(p) for k, p in both.items()} for j, both in rights.items()}
    body = functools.partial(panels_kernel, stage, left_refs, right_refs, len(arrays))
    smem = pl.BlockSpec(memory_space=pltpu.SMEM)
    hbm = pl.BlockSpec(memory_space=pl.ANY)
    vmem = pl.BlockSpec(memory_space=pltpu.VMEM)
    first, last = stage == 0, stage == STAGES - 1
    args = arrays + ([] if first else [before])
    return pl.pallas_call(
        body,
        out_shape=jax.ShapeDtypeStruct((ROWS if last else ROWS + BS, BS), F32),
        in_specs=[smem] + [hbm] * len(arrays) + [vmem] * (not first),
        out_specs=hbm if last else vmem,
        input_output_aliases={} if first or last else {1 + len(arrays): 0},
        scratch_shapes=[
            pltpu.VMEM((2, ROWS, BS), F32),
            pltpu.VMEM((2, 2 * ROWS, BS), F32),
            pltpu.SMEM((2, EXTRA, BS), F32),
            pltpu.SMEM((2, 2, EXTRA, BS), F32),
            pltpu.SMEM((HALF * 16,), jnp.int32),
            pltpu.SMEM((HALF * SLOTS * SLOTS + GROUP,), jnp.int32),
            pltpu.SemaphoreType.DMA((2, 4)),
            pltpu.SemaphoreType.DMA((2, 3)),
        ]
        + [pltpu.VMEM((ROWS + BS, BS), F32)] * last,
        compiler_params=pltpu.CompilerParams(vmem_limit_bytes=16 << 20),
        cost_estimate=pl.CostEstimate(
            flops=panels * 400_000_000, bytes_accessed=panels * 5_000_000, transcendentals=0
        ),
    )(meta, *args)


def pieces(*arrays):
    out, at = [], 0
    for n, (array, rows) in enumerate(arrays):
        out.append((array, 0, rows, at, n == len(arrays) - 1))
        at += rows
    return out


def per_device(x_blocks, x_cols, c_cols):
    columns = jnp.pad(
        x_cols.reshape(1, HALF * SLOTS).astype(F32), ((0, EXTRA - 1), (0, BS - HALF * SLOTS))
    )
    blocks = x_blocks.reshape(ROWS, BS)
    own = jnp.concatenate([blocks, columns], 0)
    own_a, own_b = jnp.concatenate([blocks[:CUT], columns], 0), own[CUT:]
    place = lax.axis_index(AXES)
    meta = lax.dynamic_index_in_dim(jnp.asarray(panel_table()), place, 0, keepdims=False)

    def swap(value):
        return move(value, d_flip=1)

    other = swap(own)
    z1, z2 = move(own, dz=1), move(other, dz=1)
    x1, x2 = move(own, dx=1), move(other, dx=1)
    z3, x3 = move(z1, dz=1), move(x1, dx=1)
    left = move(own, y_flip=2)
    ya, yb = move(own_a, y_flip=1), move(own_b, y_flip=1)
    sa, sb = swap(ya), swap(yb)
    Z1, Z2 = move(left, dz=1), move(swap(left), dz=1)
    X1, X2 = move(ya, dx=1), move(sa, dx=1)
    U1, U2 = move(yb, dx=1), move(sb, dx=1)
    ez, Z3 = move(z3[:THIRD], y_flip=2), move(Z1[THIRD:], dz=1)
    ex, X3 = move(x3[CUT:], y_flip=1), move(X1, dx=1)
    left_arrays = ((own,), (z1,), (swap(z2),), (z3,), (left,), (Z1,), (swap(Z2),), (ez, Z3))
    right_arrays = (
        ((own,), (other,)),
        ((x1,), (x2,)),
        ((swap(x2),), (swap(x1),)),
        ((x3,), (swap(x3),)),
        ((ya, yb), (sa, sb)),
        ((X1,), (X2,)),
        ((U1,), (U2,)),
        ((swap(X2),), (swap(X1),)),
        ((swap(U2),), (swap(U1),)),
        ((X3, ex), (swap(X3), swap(ex))),
    )

    def right_pieces(arrays, j):
        if len(arrays) == 2:
            return pieces(*((v, CUT) for v in arrays))
        if j < 4:
            return pieces((arrays[0], ROWS))
        return [(arrays[0], 0, CUT, CUT * (j in (6, 8)), True)]

    lefts = {
        j: pieces(*((v, min(v.shape[0], ROWS) - EXTRA * (v is Z3)) for v in arrays))
        for j, arrays in enumerate(left_arrays)
    }
    rights = {
        j: {(j, mine): right_pieces(v, j) for mine, v in enumerate(both)}
        for j, both in enumerate(right_arrays)
    }
    meta = gate(gate_kernel, gate(table_kernel, meta, c_cols))
    total = None
    for stage in range(STAGES):
        total = add_panels(
            stage,
            {j: v for j, v in lefts.items() if LEFT_STAGE[j] <= stage},
            {j: v for j, v in rights.items() if RIGHT_STAGE[j] <= stage},
            total,
            meta,
            1,
        )
    return total.reshape(HALF, SLOTS, BS, BS)


def solution(mesh):
    return jax.shard_map(
        per_device,
        mesh=mesh,
        in_specs=(
            P(("row", "depth"), "col", None, None),
            P(("row", "depth"), "col"),
            P(("row", "depth"), "col"),
        ),
        out_specs=P(("row", "depth"), "col", None, None),
        check_vma=False,
    )
```

time: 224 us -> 244 us (1.089)
  Pallas kernels: 32.1 us -> 44.7 us
  waiting for transfers between devices: 101 us -> 108 us
  local copies, waits for them, and re-layouts: 37.9 us -> 32.1 us
  starting transfers between devices: 49.7 us -> 55.4 us
    pallas_call x5 -> x11, Pallas kernels: 32.1 us -> 44.7 us  [the longest x9 41.6 us: add_panels(): pl.pallas_call(body, out_shape=jax.ShapeDtypeStruct((ROWS if last else RO...]
    ppermute x28 -> x34, waiting for transfers between devices: 101 us -> 108 us  [move(): return lax.ppermute(value, AXES, pairs)]
    ppermute x28 -> x34, starting transfers between devices: 49.7 us -> 55.4 us  [move(): return lax.ppermute(value, AXES, pairs)]
    unnamed x81 -> x99, local copies, waits for them, and re-layouts: 33.1 us -> 27.5 us
  transfers between devices with their start and end apart: 28 -> 34, of which waited for: 9 -> 9; matrix products, arithmetic and copies ran while one was open for 2% -> 2% of each run, Pallas kernels for 12% -> 16%
where the time goes in v2:
time: 244 us; the launch traced here: 242 us
  waiting for transfers between devices  108 us (44%)
  starting transfers between devices  55.4 us (23%)
  Pallas kernels  44.7 us (18%)
  local copies, waits for them, and re-layouts  32.1 us (13%)
    ppermute x34, waiting for transfers between devices, move(): return lax.ppermute(value, AXES, pairs)  108 us
    ppermute x34, starting transfers between devices, move(): return lax.ppermute(value, AXES, pairs)  55.4 us
    pallas_call x9, Pallas kernels, add_panels(): pl.pallas_call(body, out_shape=jax.ShapeDtypeStruct((ROWS if last else RO...  41.6 us
    unnamed x99, local copies, waits for them, and re-layouts  27.5 us
  transfers between devices with their start and end apart: 34, of which 9 were waited for; matrix products, arithmetic and copies ran while one was open for 2% of the time, Pallas kernels for 16%

profile of v2, /device:TPU:1, one launch (start us, length us, event | category | flops | bytes accessed | tf_op | source)
XLA Modules:
  0.0 241.7 jit_solution(8029527289473097262)
XLA Ops:
  2.3 2.2 collective-permute-start.18
  5.6 2.5 %collective-permute-start.12 = (f32[3080,128]{1,0:T(8,128)S(1)}, f32[3080,128]{1,0:T(8,128)S(1)}, u32[]{:S(2)}, u32[]{:S(2)}) collective-permute-start(f32[3080,128]{1,0:T(8,128)S(1)} %pad_maximum_fusion.refs_0_), channel_id=1, source_target_pairs={{0,16},{1,49},{2,18},{3,51},{4,20},{5,53},{6,22},{7,55},{64,80},{6... | collective-permute-start | bytes 4730888 | tf_op jit(solution)/shard_map/ppermute | solution.py:45
  8.1 3.8 %collective-permute-start = (f32[3080,128]{1,0:T(8,128)S(1)}, f32[3080,128]{1,0:T(8,128)S(1)}, u32[]{:S(2)}, u32[]{:S(2)}) collective-permute-start(f32[3080,128]{1,0:T(8,128)S(1)} %pad_maximum_fusion.refs_0_), channel_id=1, source_target_pairs={{0,2},{1,7},{2,4},{3,1},{4,6},{5,3},{6,0},{7,5},{64,66},{65,71},{6... | collective-permute-start | bytes 4730888 | tf_op jit(solution)/shard_map/ppermute | solution.py:45
  12.0 9.5 %collective-permute-done.18.refs_13_.refs_14_.refs_16_ = f32[1544,128]{1,0:T(8,128)S(1)} collective-permute-done((f32[1544,128]{1,0:T(8,128)S(1)}, f32[1544,128]{1,0:T(8,128)S(1)}, u32[]{:S(2)}, u32[]{:S(2)}) %collective-permute-start.18) | collective-permute-done | bytes 790560 | tf_op jit(solution)/shard_map/ppermute | solution.py:45
  21.5 3.1 %collective-permute-start.5 = (f32[3080,128]{1,0:T(8,128)S(1)}, f32[3080,128]{1,0:T(8,128)S(1)}, u32[]{:S(2)}, u32[]{:S(2)}) collective-permute-start(f32[3080,128]{1,0:T(8,128)S(1)} %pad_maximum_fusion.refs_0_), channel_id=1, source_target_pairs={{0,8},{1,9},{2,10},{3,11},{4,12},{5,13},{6,14},{7,15},{64,72},{65,... | collective-permute-start | bytes 4730888 | tf_op jit(solution)/shard_map/ppermute | solution.py:45
  24.6 13.8 %collective-permute-done.19.refs_14_.refs_15_.refs_17_ = f32[1544,128]{1,0:T(8,128)S(1)} collective-permute-done((f32[1544,128]{1,0:T(8,128)S(1)}, f32[1544,128]{1,0:T(8,128)S(1)}, u32[]{:S(2)}, u32[]{:S(2)}) %collective-permute-start.19) | collective-permute-done | bytes 790560 | tf_op jit(solution)/shard_map/ppermute | solution.py:45
  38.4 2.8 %collective-permute-start.20 = (f32[1544,128]{1,0:T(8,128)S(1)}, f32[1544,128]{1,0:T(8,128)S(1)}, u32[]{:S(2)}, u32[]{:S(2)}) collective-permute-start(f32[1544,128]{1,0:T(8,128)S(1)} %collective-permute-done.18.refs_13_.refs_14_.refs_16_), channel_id=1, source_target_pairs={{0,1},{1,0},{2,3},{3,2},{4,5},{5,4},{6,7},{7,6},{64,65},{65,64},{6... | collective-permute-start | bytes 2371592 | tf_op jit(solution)/shard_map/ppermute | solution.py:45
  41.2 2.6 %collective-permute-start.22 = (f32[1544,128]{1,0:T(8,128)S(1)}, f32[1544,128]{1,0:T(8,128)S(1)}, u32[]{:S(2)}, u32[]{:S(2)}) collective-permute-start(f32[1544,128]{1,0:T(8,128)S(1)} %collective-permute-done.18.refs_13_.refs_14_.refs_16_), channel_id=1, source_target_pairs={{0,16},{1,49},{2,18},{3,51},{4,20},{5,53},{6,22},{7,55},{64,80},{6... | collective-permute-start | bytes 2371592 | tf_op jit(solution)/shard_map/ppermute | solution.py:45
  48.3 26.6 %collective-permute-done.5.refs_3_.refs_4_ = f32[3080,128]{1,0:T(8,128)S(1)} collective-permute-done((f32[3080,128]{1,0:T(8,128)S(1)}, f32[3080,128]{1,0:T(8,128)S(1)}, u32[]{:S(2)}, u32[]{:S(2)}) %collective-permute-start.5) | collective-permute-done | bytes 1576992 | tf_op jit(solution)/shard_map/ppermute | solution.py:45
  74.9 2.5 %collective-permute-start.13 = (f32[3080,128]{1,0:T(8,128)S(1)}, f32[3080,128]{1,0:T(8,128)S(1)}, u32[]{:S(2)}, u32[]{:S(2)}) collective-permute-start(f32[3080,128]{1,0:T(8,128)S(1)} %collective-permute-done.1.refs_2_.refs_4_.refs_6_.refs_7_.refs_9_), channel_id=1, source_target_pairs={{0,16},{1,49},{2,18},{3,51},{4,20},{5,53},{6,22},{7,55},{64,80},{6... | collective-permute-start | bytes 4730888 | tf_op jit(solution)/shard_map/ppermute | solution.py:45
  80.4 3.8 %collective-permute-start.2 = (f32[3080,128]{1,0:T(8,128)S(1)}, f32[3080,128]{1,0:T(8,128)S(1)}, u32[]{:S(2)}, u32[]{:S(2)}) collective-permute-start(f32[3080,128]{1,0:T(8,128)S(1)} %collective-permute-done.1.refs_2_.refs_4_.refs_6_.refs_7_.refs_9_), channel_id=1, source_target_pairs={{0,2},{1,7},{2,4},{3,1},{4,6},{5,3},{6,0},{7,5},{64,66},{65,71},{6... | collective-permute-start | bytes 4730888 | tf_op jit(solution)/shard_map/ppermute | solution.py:45
  87.2 16.1 %collective-permute-done.30.refs_21_.refs_22_.refs_24_.refs_28_ = f32[1544,128]{1,0:T(8,128)S(1)} collective-permute-done((f32[1544,128]{1,0:T(8,128)S(1)}, f32[1544,128]{1,0:T(8,128)S(1)}, u32[]{:S(2)}, u32[]{:S(2)}) %collective-permute-start.30) | collective-permute-done | bytes 790560 | tf_op jit(solution)/shard_map/ppermute | solution.py:45
  103.3 3.3 %collective-permute-start.15 = (f32[3080,128]{1,0:T(8,128)S(1)}, f32[3080,128]{1,0:T(8,128)S(1)}, u32[]{:S(2)}, u32[]{:S(2)}) collective-permute-start(f32[3080,128]{1,0:T(8,128)S(1)} %collective-permute-done.12.refs_3_.refs_5_.refs_7_.refs_8_.refs_10_), channel_id=1, source_target_pairs={{0,1},{1,0},{2,3},{3,2},{4,5},{5,4},{6,7},{7,6},{64,65},{65,64},{6... | collective-permute-start | bytes 4730888 | tf_op jit(solution)/shard_map/ppermute | solution.py:45
  106.6 5.2 %collective-permute-done.25.refs_23_ = f32[1544,128]{1,0:T(8,128)} collective-permute-done((f32[1544,128]{1,0:T(8,128)S(1)}, f32[1544,128]{1,0:T(8,128)}, u32[]{:S(2)}, u32[]{:S(2)}) %collective-permute-start.25) | collective-permute-done | bytes 790560 | tf_op jit(solution)/shard_map/ppermute | solution.py:45
  111.7 3.2 %collective-permute-start.16 = (f32[3080,128]{1,0:T(8,128)S(1)}, f32[3080,128]{1,0:T(8,128)S(1)}, u32[]{:S(2)}, u32[]{:S(2)}) collective-permute-start(f32[3080,128]{1,0:T(8,128)S(1)} %collective-permute-done.12.refs_3_.refs_5_.refs_7_.refs_8_.refs_10_), channel_id=1, source_target_pairs={{0,16},{1,49},{2,18},{3,51},{4,20},{5,53},{6,22},{7,55},{64,80},{6... | collective-permute-start | bytes 4730888 | tf_op jit(solution)/shard_map/ppermute | solution.py:45
  116.1 3.8 %collective-permute-start.4 = (f32[3080,128]{1,0:T(8,128)S(1)}, f32[3080,128]{1,0:T(8,128)S(1)}, u32[]{:S(2)}, u32[]{:S(2)}) collective-permute-start(f32[3080,128]{1,0:T(8,128)S(1)} %collective-permute-done.refs_1_), channel_id=1, source_target_pairs={{0,2},{1,7},{2,4},{3,1},{4,6},{5,3},{6,0},{7,5},{64,66},{65,71},{6... | collective-permute-start | bytes 4730888 | tf_op jit(solution)/shard_map/ppermute | solution.py:45
  123.6 2.1 collective-permute-start.26
  126.5 5.8 %collective-permute-done.16.refs_11_.refs_12_.refs_14_ = f32[3080,128]{1,0:T(8,128)S(1)} collective-permute-done((f32[3080,128]{1,0:T(8,128)S(1)}, f32[3080,128]{1,0:T(8,128)S(1)}, u32[]{:S(2)}, u32[]{:S(2)}) %collective-permute-start.16) | collective-permute-done | bytes 1576992 | tf_op jit(solution)/shard_map/ppermute | solution.py:45
  132.4 4.5 %collective-permute-start.32 = (f32[1544,128]{1,0:T(8,128)S(1)}, f32[1544,128]{1,0:T(8,128)S(1)}, u32[]{:S(2)}, u32[]{:S(2)}) collective-permute-start(f32[1544,128]{1,0:T(8,128)S(1)} %collective-permute-done.30.refs_21_.refs_22_.refs_24_.refs_28_), channel_id=1, source_target_pairs={{0,1},{1,0},{2,3},{3,2},{4,5},{5,4},{6,7},{7,6},{64,65},{65,64},{6... | collective-permute-start | bytes 2371592 | tf_op jit(solution)/shard_map/ppermute | solution.py:45
  140.2 14.0 %collective-permute-done.6.refs_5_ = f32[3080,128]{1,0:T(8,128)S(1)} collective-permute-done((f32[3080,128]{1,0:T(8,128)S(1)}, f32[3080,128]{1,0:T(8,128)S(1)}, u32[]{:S(2)}, u32[]{:S(2)}) %collective-permute-start.6) | collective-permute-done | bytes 1576992 | tf_op jit(solution)/shard_map/ppermute | solution.py:45
  159.1 11.9 %collective-permute-done.8 = f32[3080,128]{1,0:T(8,128)} collective-permute-done((f32[3080,128]{1,0:T(8,128)S(1)}, f32[3080,128]{1,0:T(8,128)}, u32[]{:S(2)}, u32[]{:S(2)}) %collective-permute-start.8) | collective-permute-done | bytes 1576992 | tf_op jit(solution)/shard_map/ppermute | solution.py:45
  171.0 1.9 collective-permute-start.9
  172.9 4.9 %collective-permute-done.31.refs_22_.refs_23_.refs_25_.refs_29_ = f32[1544,128]{1,0:T(8,128)S(1)} collective-permute-done((f32[1544,128]{1,0:T(8,128)S(1)}, f32[1544,128]{1,0:T(8,128)S(1)}, u32[]{:S(2)}, u32[]{:S(2)}) %collective-permute-start.31) | collective-permute-done | bytes 790560 | tf_op jit(solution)/shard_map/ppermute | solution.py:45
  181.4 1.9 collective-permute-start.11
  199.4 7.1 %shard_map.48.refs_9_ = f32[3200,128]{1,0:T(8,128)S(1)} custom-call(s32[15,18]{1,0:T(8,128)S(1)} %copy-done.46, f32[3080,128]{1,0:T(8,128)S(1)} %pad_maximum_fusion.refs_0_, f32[3080,128]{1,0:T(8,128)S(1)} %copy-done.3, f32[3080,128]{1,0:T(8,128)S(1)} %collective-permute-done.1.refs_2_.refs_4_.refs_6_.refs_7_.refs_9_, f32[3080,128]{1,0:T(8,128)S(1)} %copy-done.1, ...), custom_call_target="tpu_custom_call" | custom-call | flops 400000000 | bytes 5000000 | tf_op jit(solution)/shard_map/pallas_call | solution.py:260
  206.7 4.5 %shard_map.49.refs_13_ = f32[3200,128]{1,0:T(8,128)S(1)} custom-call(s32[15,18]{1,0:T(8,128)S(1)} %copy-done.46, f32[3080,128]{1,0:T(8,128)S(1)} %pad_maximum_fusion.refs_0_, f32[3080,128]{1,0:T(8,128)S(1)} %copy-done.3, f32[3080,128]{1,0:T(8,128)S(1)} %copy-done.13, f32[3080,128]{1,0:T(8,128)S(1)} %copy-done.7, ...), custom_call_target="tpu_custom_call", output_to_operand_aliasing={{}: (10, {})} | custom-call | flops 400000000 | bytes 5000000 | tf_op jit(solution)/shard_map/pallas_call | solution.py:260
  211.2 4.5 %shard_map.50.refs_17_ = f32[3200,128]{1,0:T(8,128)S(1)} custom-call(s32[15,18]{1,0:T(8,128)S(1)} %copy-done.46, f32[3080,128]{1,0:T(8,128)S(1)} %pad_maximum_fusion.refs_0_, f32[3080,128]{1,0:T(8,128)S(1)} %copy-done.3, f32[3080,128]{1,0:T(8,128)S(1)} %copy-done.13, f32[3080,128]{1,0:T(8,128)S(1)} %copy-done.19, ...), custom_call_target="tpu_custom_call", output_to_operand_aliasing={{}: (14, {})} | custom-call | flops 400000000 | bytes 5000000 | tf_op jit(solution)/shard_map/pallas_call | solution.py:260
  215.7 4.8 %shard_map.51.refs_21_ = f32[3200,128]{1,0:T(8,128)S(1)} custom-call(s32[15,18]{1,0:T(8,128)S(1)} %copy-done.46, f32[3080,128]{1,0:T(8,128)S(1)} %pad_maximum_fusion.refs_0_, f32[3080,128]{1,0:T(8,128)S(1)} %copy-done.3, f32[3080,128]{1,0:T(8,128)S(1)} %copy-done.13, f32[3080,128]{1,0:T(8,128)S(1)} %copy-done.19, ...), custom_call_target="tpu_custom_call", output_to_operand_aliasing={{}: (18, {})} | custom-call | flops 400000000 | bytes 5000000 | tf_op jit(solution)/shard_map/pallas_call | solution.py:260
  220.6 4.1 %shard_map.52.refs_25_ = f32[3200,128]{1,0:T(8,128)S(1)} custom-call(s32[15,18]{1,0:T(8,128)S(1)} %copy-done.46, f32[3080,128]{1,0:T(8,128)S(1)} %pad_maximum_fusion.refs_0_, f32[3080,128]{1,0:T(8,128)S(1)} %copy-done.3, f32[3080,128]{1,0:T(8,128)S(1)} %copy-done.13, f32[3080,128]{1,0:T(8,128)S(1)} %copy-done.19, ...), custom_call_target="tpu_custom_call", output_to_operand_aliasing={{}: (22, {})} | custom-call | flops 400000000 | bytes 5000000 | tf_op jit(solution)/shard_map/pallas_call | solution.py:260
  225.8 4.0 %shard_map.54.refs_28_ = f32[3200,128]{1,0:T(8,128)S(1)} custom-call(s32[15,18]{1,0:T(8,128)S(1)} %copy-done.46, f32[3080,128]{1,0:T(8,128)S(1)} %pad_maximum_fusion.refs_0_, f32[3080,128]{1,0:T(8,128)S(1)} %copy-done.3, f32[3080,128]{1,0:T(8,128)S(1)} %copy-done.13, f32[3080,128]{1,0:T(8,128)S(1)} %copy-done.19, ...), custom_call_target="tpu_custom_call", output_to_operand_aliasing={{}: (27, {})} | custom-call | flops 400000000 | bytes 5000000 | tf_op jit(solution)/shard_map/pallas_call | solution.py:260
  229.8 4.7 %shard_map.55.refs_32_ = f32[3200,128]{1,0:T(8,128)S(1)} custom-call(s32[15,18]{1,0:T(8,128)S(1)} %copy-done.46, f32[3080,128]{1,0:T(8,128)S(1)} %pad_maximum_fusion.refs_0_, f32[3080,128]{1,0:T(8,128)S(1)} %copy-done.3, f32[3080,128]{1,0:T(8,128)S(1)} %copy-done.13, f32[3080,128]{1,0:T(8,128)S(1)} %copy-done.19, ...), custom_call_target="tpu_custom_call", output_to_operand_aliasing={{}: (29, {})} | custom-call | flops 400000000 | bytes 5000000 | tf_op jit(solution)/shard_map/pallas_call | solution.py:260
  234.5 7.0 %shard_map.56 = f32[3072,128]{1,0:T(8,128)} custom-call(s32[15,18]{1,0:T(8,128)S(1)} %copy-done.46, f32[3080,128]{1,0:T(8,128)S(1)} %pad_maximum_fusion.refs_0_, f32[3080,128]{1,0:T(8,128)S(1)} %copy-done.3, f32[3080,128]{1,0:T(8,128)S(1)} %copy-done.13, f32[3080,128]{1,0:T(8,128)S(1)} %copy-done.19, f32[3080,128]{1,0:T(8,128)S(1)} %copy-done.7, ...), custom_call_target="tpu_custom_call" | custom-call | flops 400000000 | bytes 5000000 | tf_op jit(solution)/shard_map/pallas_call | solution.py:260
  (157 shorter events, 49.0 us)
Async XLA Ops:
  2.3 19.2 %collective-permute-start.18 = (f32[1544,128]{1,0:T(8,128)S(1)}, f32[1544,128]{1,0:T(8,128)S(1)}, u32[]{:S(2)}, u32[]{:S(2)}) collective-permute-start(f32[1544,128]{1,0:T(8,128)S(1)} %get-tuple-element.6), channel_id=1, source_target_pairs={{0,64},{1,65},{2,66},{3,67},{4,68},{5,69},{6,70},{7,71},{64,0},{65... | collective-permute-start | bytes 2371592 | tf_op jit(solution)/shard_map/ppermute | solution.py:45
  4.6 36.6 %collective-permute-start.1 = (f32[3080,128]{1,0:T(8,128)S(1)}, f32[3080,128]{1,0:T(8,128)S(1)}, u32[]{:S(2)}, u32[]{:S(2)}) collective-permute-start(f32[3080,128]{1,0:T(8,128)S(1)} %pad_maximum_fusion.refs_0_), channel_id=1, source_target_pairs={{0,1},{1,0},{2,3},{3,2},{4,5},{5,4},{6,7},{7,6},{64,65},{65,64},{6... | collective-permute-start | bytes 4730888 | tf_op jit(solution)/shard_map/ppermute | solution.py:45
  5.6 39.1 %collective-permute-start.12 = (f32[3080,128]{1,0:T(8,128)S(1)}, f32[3080,128]{1,0:T(8,128)S(1)}, u32[]{:S(2)}, u32[]{:S(2)}) collective-permute-start(f32[3080,128]{1,0:T(8,128)S(1)} %pad_maximum_fusion.refs_0_), channel_id=1, source_target_pairs={{0,16},{1,49},{2,18},{3,51},{4,20},{5,53},{6,22},{7,55},{64,80},{6... | collective-permute-start | bytes 4730888 | tf_op jit(solution)/shard_map/ppermute | solution.py:45
  8.1 36.7 %collective-permute-start = (f32[3080,128]{1,0:T(8,128)S(1)}, f32[3080,128]{1,0:T(8,128)S(1)}, u32[]{:S(2)}, u32[]{:S(2)}) collective-permute-start(f32[3080,128]{1,0:T(8,128)S(1)} %pad_maximum_fusion.refs_0_), channel_id=1, source_target_pairs={{0,2},{1,7},{2,4},{3,1},{4,6},{5,3},{6,0},{7,5},{64,66},{65,71},{6... | collective-permute-start | bytes 4730888 | tf_op jit(solution)/shard_map/ppermute | solution.py:45
  11.9 26.6 %collective-permute-start.19 = (f32[1544,128]{1,0:T(8,128)S(1)}, f32[1544,128]{1,0:T(8,128)S(1)}, u32[]{:S(2)}, u32[]{:S(2)}) collective-permute-start(f32[1544,128]{1,0:T(8,128)S(1)} %get-tuple-element.5), channel_id=1, source_target_pairs={{0,64},{1,65},{2,66},{3,67},{4,68},{5,69},{6,70},{7,71},{64,0},{65... | collective-permute-start | bytes 2371592 | tf_op jit(solution)/shard_map/ppermute | solution.py:45
  21.5 53.4 %collective-permute-start.5 = (f32[3080,128]{1,0:T(8,128)S(1)}, f32[3080,128]{1,0:T(8,128)S(1)}, u32[]{:S(2)}, u32[]{:S(2)}) collective-permute-start(f32[3080,128]{1,0:T(8,128)S(1)} %pad_maximum_fusion.refs_0_), channel_id=1, source_target_pairs={{0,8},{1,9},{2,10},{3,11},{4,12},{5,13},{6,14},{7,15},{64,72},{65,... | collective-permute-start | bytes 4730888 | tf_op jit(solution)/shard_map/ppermute | solution.py:45
  41.2 36.2 %collective-permute-start.22 = (f32[1544,128]{1,0:T(8,128)S(1)}, f32[1544,128]{1,0:T(8,128)S(1)}, u32[]{:S(2)}, u32[]{:S(2)}) collective-permute-start(f32[1544,128]{1,0:T(8,128)S(1)} %collective-permute-done.18.refs_13_.refs_14_.refs_16_), channel_id=1, source_target_pairs={{0,16},{1,49},{2,18},{3,51},{4,20},{5,53},{6,22},{7,55},{64,80},{6... | collective-permute-start | bytes 2371592 | tf_op jit(solution)/shard_map/ppermute | solution.py:45
  44.8 33.2 %collective-permute-start.21 = (f32[1544,128]{1,0:T(8,128)S(1)}, f32[1544,128]{1,0:T(8,128)S(1)}, u32[]{:S(2)}, u32[]{:S(2)}) collective-permute-start(f32[1544,128]{1,0:T(8,128)S(1)} %collective-permute-done.19.refs_14_.refs_15_.refs_17_), channel_id=1, source_target_pairs={{0,1},{1,0},{2,3},{3,2},{4,5},{5,4},{6,7},{7,6},{64,65},{65,64},{6... | collective-permute-start | bytes 2371592 | tf_op jit(solution)/shard_map/ppermute | solution.py:45
  44.8 35.6 %collective-permute-start.24 = (f32[1544,128]{1,0:T(8,128)S(1)}, f32[1544,128]{1,0:T(8,128)}, u32[]{:S(2)}, u32[]{:S(2)}) collective-permute-start(f32[1544,128]{1,0:T(8,128)S(1)} %collective-permute-done.19.refs_14_.refs_15_.refs_17_), channel_id=1, source_target_pairs={{0,16},{1,49},{2,18},{3,51},{4,20},{5,53},{6,22},{7,55},{64,80},{6... | collective-permute-start | bytes 2371592 | tf_op jit(solution)/shard_map/ppermute | solution.py:45
  46.3 37.9 %collective-permute-start.23 = (f32[1544,128]{1,0:T(8,128)S(1)}, f32[1544,128]{1,0:T(8,128)S(1)}, u32[]{:S(2)}, u32[]{:S(2)}) collective-permute-start(f32[1544,128]{1,0:T(8,128)S(1)} %collective-permute-done.20.refs_15_.refs_16_.refs_18_), channel_id=1, source_target_pairs={{0,16},{1,49},{2,18},{3,51},{4,20},{5,53},{6,22},{7,55},{64,80},{6... | collective-permute-start | bytes 2371592 | tf_op jit(solution)/shard_map/ppermute | solution.py:45
  74.9 41.2 %collective-permute-start.13 = (f32[3080,128]{1,0:T(8,128)S(1)}, f32[3080,128]{1,0:T(8,128)S(1)}, u32[]{:S(2)}, u32[]{:S(2)}) collective-permute-start(f32[3080,128]{1,0:T(8,128)S(1)} %collective-permute-done.1.refs_2_.refs_4_.refs_6_.refs_7_.refs_9_), channel_id=1, source_target_pairs={{0,16},{1,49},{2,18},{3,51},{4,20},{5,53},{6,22},{7,55},{64,80},{6... | collective-permute-start | bytes 4730888 | tf_op jit(solution)/shard_map/ppermute | solution.py:45
  77.9 25.3 %collective-permute-start.30 = (f32[1544,128]{1,0:T(8,128)S(1)}, f32[1544,128]{1,0:T(8,128)S(1)}, u32[]{:S(2)}, u32[]{:S(2)}) collective-permute-start(f32[1544,128]{1,0:T(8,128)S(1)} %collective-permute-done.22.refs_17_.refs_18_.refs_20_), channel_id=1, source_target_pairs={{0,16},{1,49},{2,18},{3,51},{4,20},{5,53},{6,22},{7,55},{64,80},{6... | collective-permute-start | bytes 2371592 | tf_op jit(solution)/shard_map/ppermute | solution.py:45
  80.4 40.7 %collective-permute-start.2 = (f32[3080,128]{1,0:T(8,128)S(1)}, f32[3080,128]{1,0:T(8,128)S(1)}, u32[]{:S(2)}, u32[]{:S(2)}) collective-permute-start(f32[3080,128]{1,0:T(8,128)S(1)} %collective-permute-done.1.refs_2_.refs_4_.refs_6_.refs_7_.refs_9_), channel_id=1, source_target_pairs={{0,2},{1,7},{2,4},{3,1},{4,6},{5,3},{6,0},{7,5},{64,66},{65,71},{6... | collective-permute-start | bytes 4730888 | tf_op jit(solution)/shard_map/ppermute | solution.py:45
  84.1 27.6 %collective-permute-start.25 = (f32[1544,128]{1,0:T(8,128)S(1)}, f32[1544,128]{1,0:T(8,128)}, u32[]{:S(2)}, u32[]{:S(2)}) collective-permute-start(f32[1544,128]{1,0:T(8,128)S(1)} %collective-permute-done.21.refs_16_.refs_17_.refs_19_), channel_id=1, source_target_pairs={{0,16},{1,49},{2,18},{3,51},{4,20},{5,53},{6,22},{7,55},{64,80},{6... | collective-permute-start | bytes 2371592 | tf_op jit(solution)/shard_map/ppermute | solution.py:45
  87.2 35.2 %collective-permute-start.7 = (f32[3080,128]{1,0:T(8,128)S(1)}, f32[3080,128]{1,0:T(8,128)S(1)}, u32[]{:S(2)}, u32[]{:S(2)}) collective-permute-start(f32[3080,128]{1,0:T(8,128)S(1)} %collective-permute-done.5.refs_3_.refs_4_), channel_id=1, source_target_pairs={{0,1},{1,0},{2,3},{3,2},{4,5},{5,4},{6,7},{7,6},{64,65},{65,64},{6... | collective-permute-start | bytes 4730888 | tf_op jit(solution)/shard_map/ppermute | solution.py:45
  103.3 19.1 %collective-permute-start.15 = (f32[3080,128]{1,0:T(8,128)S(1)}, f32[3080,128]{1,0:T(8,128)S(1)}, u32[]{:S(2)}, u32[]{:S(2)}) collective-permute-start(f32[3080,128]{1,0:T(8,128)S(1)} %collective-permute-done.12.refs_3_.refs_5_.refs_7_.refs_8_.refs_10_), channel_id=1, source_target_pairs={{0,1},{1,0},{2,3},{3,2},{4,5},{5,4},{6,7},{7,6},{64,65},{65,64},{6... | collective-permute-start | bytes 4730888 | tf_op jit(solution)/shard_map/ppermute | solution.py:45
  111.7 20.6 %collective-permute-start.16 = (f32[3080,128]{1,0:T(8,128)S(1)}, f32[3080,128]{1,0:T(8,128)S(1)}, u32[]{:S(2)}, u32[]{:S(2)}) collective-permute-start(f32[3080,128]{1,0:T(8,128)S(1)} %collective-permute-done.12.refs_3_.refs_5_.refs_7_.refs_8_.refs_10_), channel_id=1, source_target_pairs={{0,16},{1,49},{2,18},{3,51},{4,20},{5,53},{6,22},{7,55},{64,80},{6... | collective-permute-start | bytes 4730888 | tf_op jit(solution)/shard_map/ppermute | solution.py:45
  116.1 21.7 %collective-permute-start.4 = (f32[3080,128]{1,0:T(8,128)S(1)}, f32[3080,128]{1,0:T(8,128)S(1)}, u32[]{:S(2)}, u32[]{:S(2)}) collective-permute-start(f32[3080,128]{1,0:T(8,128)S(1)} %collective-permute-done.refs_1_), channel_id=1, source_target_pairs={{0,2},{1,7},{2,4},{3,1},{4,6},{5,3},{6,0},{7,5},{64,66},{65,71},{6... | collective-permute-start | bytes 4730888 | tf_op jit(solution)/shard_map/ppermute | solution.py:45
  121.1 33.1 %collective-permute-start.6 = (f32[3080,128]{1,0:T(8,128)S(1)}, f32[3080,128]{1,0:T(8,128)S(1)}, u32[]{:S(2)}, u32[]{:S(2)}) collective-permute-start(f32[3080,128]{1,0:T(8,128)S(1)} %collective-permute-done.5.refs_3_.refs_4_), channel_id=1, source_target_pairs={{0,2},{1,7},{2,4},{3,1},{4,6},{5,3},{6,0},{7,5},{64,66},{65,71},{6... | collective-permute-start | bytes 4730888 | tf_op jit(solution)/shard_map/ppermute | solution.py:45
  122.4 48.7 %collective-permute-start.8 = (f32[3080,128]{1,0:T(8,128)S(1)}, f32[3080,128]{1,0:T(8,128)}, u32[]{:S(2)}, u32[]{:S(2)}) collective-permute-start(f32[3080,128]{1,0:T(8,128)S(1)} %collective-permute-done.7), channel_id=1, source_target_pairs={{0,2},{1,7},{2,4},{3,1},{4,6},{5,3},{6,0},{7,5},{64,66},{65,71},{6... | collective-permute-start | bytes 4730888 | tf_op jit(solution)/shard_map/ppermute | solution.py:45
  123.6 32.4 %collective-permute-start.26 = (f32[1544,128]{1,0:T(8,128)S(1)}, f32[1544,128]{1,0:T(8,128)S(1)}, u32[]{:S(2)}, u32[]{:S(2)}) collective-permute-start(f32[1544,128]{1,0:T(8,128)S(1)} %collective-permute-done.23.refs_18_.refs_19_.refs_21_), channel_id=1, source_target_pairs={{0,1},{1,0},{2,3},{3,2},{4,5},{5,4},{6,7},{7,6},{64,65},{65,64},{6... | collective-permute-start | bytes 2371592 | tf_op jit(solution)/shard_map/ppermute | solution.py:45
  132.4 25.8 %collective-permute-start.32 = (f32[1544,128]{1,0:T(8,128)S(1)}, f32[1544,128]{1,0:T(8,128)S(1)}, u32[]{:S(2)}, u32[]{:S(2)}) collective-permute-start(f32[1544,128]{1,0:T(8,128)S(1)} %collective-permute-done.30.refs_21_.refs_22_.refs_24_.refs_28_), channel_id=1, source_target_pairs={{0,1},{1,0},{2,3},{3,2},{4,5},{5,4},{6,7},{7,6},{64,65},{65,64},{6... | collective-permute-start | bytes 2371592 | tf_op jit(solution)/shard_map/ppermute | solution.py:45
  137.8 42.4 %collective-permute-start.14 = (f32[3080,128]{1,0:T(8,128)S(1)}, f32[3080,128]{1,0:T(8,128)S(1)}, u32[]{:S(2)}, u32[]{:S(2)}) collective-permute-start(f32[3080,128]{1,0:T(8,128)S(1)} %collective-permute-done.13.refs_4_.refs_6_.refs_8_.refs_9_.refs_11_), channel_id=1, source_target_pairs={{0,1},{1,0},{2,3},{3,2},{4,5},{5,4},{6,7},{7,6},{64,65},{65,64},{6... | collective-permute-start | bytes 4730888 | tf_op jit(solution)/shard_map/ppermute | solution.py:45
  154.1 29.2 %collective-permute-start.3 = (f32[3080,128]{1,0:T(8,128)S(1)}, f32[3080,128]{1,0:T(8,128)S(1)}, u32[]{:S(2)}, u32[]{:S(2)}) collective-permute-start(f32[3080,128]{1,0:T(8,128)S(1)} %collective-permute-done.2), channel_id=1, source_target_pairs={{0,1},{1,0},{2,3},{3,2},{4,5},{5,4},{6,7},{7,6},{64,65},{65,64},{6... | collective-permute-start | bytes 4730888 | tf_op jit(solution)/shard_map/ppermute | solution.py:45
  156.9 27.6 %collective-permute-start.17 = (f32[3080,128]{1,0:T(8,128)S(1)}, f32[3080,128]{1,0:T(8,128)S(1)}, u32[]{:S(2)}, u32[]{:S(2)}) collective-permute-start(f32[3080,128]{1,0:T(8,128)S(1)} %collective-permute-done.16.refs_11_.refs_12_.refs_14_), channel_id=1, source_target_pairs={{0,1},{1,0},{2,3},{3,2},{4,5},{5,4},{6,7},{7,6},{64,65},{65,64},{6... | collective-permute-start | bytes 4730888 | tf_op jit(solution)/shard_map/ppermute | solution.py:45
  159.1 18.7 %collective-permute-start.31 = (f32[1544,128]{1,0:T(8,128)S(1)}, f32[1544,128]{1,0:T(8,128)S(1)}, u32[]{:S(2)}, u32[]{:S(2)}) collective-permute-start(f32[1544,128]{1,0:T(8,128)S(1)} %slice.28), channel_id=1, source_target_pairs={{0,64},{1,65},{2,66},{3,67},{4,68},{5,69},{6,70},{7,71},{64,0},{65... | collective-permute-start | bytes 2371592 | tf_op jit(solution)/shard_map/ppermute | solution.py:45
  171.0 54.8 %collective-permute-start.9 = (f32[3080,128]{1,0:T(8,128)}, f32[3080,128]{1,0:T(8,128)}, u32[]{:S(2)}, u32[]{:S(2)}) collective-permute-start(f32[3080,128]{1,0:T(8,128)} %collective-permute-done.8), channel_id=1, source_target_pairs={{0,1},{1,0},{2,3},{3,2},{4,5},{5,4},{6,7},{7,6},{64,65},{65,64},{6... | collective-permute-start | bytes 4730888 | tf_op jit(solution)/shard_map/ppermute | solution.py:45
  177.8 10.3 %collective-permute-start.33 = (f32[1544,128]{1,0:T(8,128)S(1)}, f32[1544,128]{1,0:T(8,128)S(1)}, u32[]{:S(2)}, u32[]{:S(2)}) collective-permute-start(f32[1544,128]{1,0:T(8,128)S(1)} %collective-permute-done.31.refs_22_.refs_23_.refs_25_.refs_29_), channel_id=1, source_target_pairs={{0,1},{1,0},{2,3},{3,2},{4,5},{5,4},{6,7},{7,6},{64,65},{65,64},{6... | collective-permute-start | bytes 2371592 | tf_op jit(solution)/shard_map/ppermute | solution.py:45
  181.4 48.4 %collective-permute-start.11 = (f32[2056,128]{1,0:T(8,128)}, f32[2056,128]{1,0:T(8,128)}, u32[]{:S(2)}, u32[]{:S(2)}) collective-permute-start(f32[2056,128]{1,0:T(8,128)} %slice.25), channel_id=1, source_target_pairs={{0,2},{1,7},{2,4},{3,1},{4,6},{5,3},{6,0},{7,5},{64,66},{65,71},{6... | collective-permute-start | bytes 3158024 | tf_op jit(solution)/shard_map/ppermute | solution.py:45
  184.5 50.0 %collective-permute-start.29 = (f32[1544,128]{1,0:T(8,128)}, f32[1544,128]{1,0:T(8,128)}, u32[]{:S(2)}, u32[]{:S(2)}) collective-permute-start(f32[1544,128]{1,0:T(8,128)} %collective-permute-done.24.refs_22_), channel_id=1, source_target_pairs={{0,1},{1,0},{2,3},{3,2},{4,5},{5,4},{6,7},{7,6},{64,65},{65,64},{6... | collective-permute-start | bytes 2371592 | tf_op jit(solution)/shard_map/ppermute | solution.py:45
  185.6 48.9 %collective-permute-start.28 = (f32[1544,128]{1,0:T(8,128)}, f32[1544,128]{1,0:T(8,128)}, u32[]{:S(2)}, u32[]{:S(2)}) collective-permute-start(f32[1544,128]{1,0:T(8,128)} %collective-permute-done.25.refs_23_), channel_id=1, source_target_pairs={{0,1},{1,0},{2,3},{3,2},{4,5},{5,4},{6,7},{7,6},{64,65},{65,64},{6... | collective-permute-start | bytes 2371592 | tf_op jit(solution)/shard_map/ppermute | solution.py:45
  189.0 40.8 %collective-permute-start.10 = (f32[1024,128]{1,0:T(8,128)}, f32[1024,128]{1,0:T(8,128)}, u32[]{:S(2)}, u32[]{:S(2)}) collective-permute-start(f32[1024,128]{1,0:T(8,128)} %slice.24), channel_id=1, source_target_pairs={{0,8},{1,9},{2,10},{3,11},{4,12},{5,13},{6,14},{7,15},{64,72},{65,... | collective-permute-start | bytes 1572872 | tf_op jit(solution)/shard_map/ppermute | solution.py:45
  (51 other events, 214.0 us)
